TPU v7x, 256 devices: a whole 4x4x8 slice. The times are simulated.
256 devices in a mesh: facet: 16 (over x, y), chan: 16 (over z, core).
Axes of the slice: x: 4, y: 4, z: 8, core: 2. Of those that a mesh axis runs over, the one named last changes fastest.
Arguments:
- visibility: float32 [4096, 2, 512], P(('facet', 'chan')), may hold values from -6 to 6
- uv_coords: float32 [4096, 2, 512], P(('facet', 'chan')), may hold values from 0 to 63
- vis_count: int32 [4096], P(('facet', 'chan')), may hold values from 256 to 512, as said below
- subgrid_facet: int32 [4096, 1], P(('facet', 'chan')), may hold values from 0 to 15; in each aligned block of 16 rows (0 to 15, 16 to 31, ...) at most 2 rows name the same one
- row_offset: int32 [4096], P(('facet', 'chan')), may hold values from 0 to 64
- col_offset: int32 [4096], P(('facet', 'chan')), may hold values from 0 to 4032
- model_facet: bfloat16 [16, 128, 2, 4096], P('facet'), may hold values from -6 to 6
Outputs:
- facet_image: float32 [16, 128, 2, 4096], P('facet', 'chan')
- residual_vis: float32 [4096, 2, 512], P(('facet', 'chan'))
Inputs may be any that keep to these rules, and one draw needn't show every extreme that they name: `subgrid_facet`: in every device's block of 16 subgrids at most 2 name the same facet, a bound that some block reaches. `vis_count`: in every device's block of 16 subgrids one subgrid has all 512 visibilities live.
All inputs are finite; a program needn't handle non-finite values.
Results may differ from a plain program's by a relative error of at most 0.012.
Values may be sent and summed in bfloat16 or wider, within the bound.
A program may use at most 64 MiB of HBM per device.

v0:
```python
import math

import jax
import jax.numpy as jnp
from jax import lax
from jax.sharding import PartitionSpec as P

SUB = 64
FACET = 4096
F_ROWS = 128
NV = 512


KERNEL_COEF = 1.0


def dft_tables(length):
    index_line = jnp.arange(length, dtype=jnp.int32)
    phase = index_line[:, None] * index_line[None, :] % length
    angle = 2.0 * math.pi * phase.astype(jnp.float32) / length
    cos_table = (jnp.cos(angle) / math.sqrt(length)).astype(jnp.bfloat16)
    sin_table = (-jnp.sin(angle) / math.sqrt(length)).astype(jnp.bfloat16)
    right_forward = jnp.concatenate(
        [jnp.concatenate([cos_table, sin_table], 1), jnp.concatenate([-sin_table, cos_table], 1)], 0
    )
    right_inverse = jnp.concatenate(
        [jnp.concatenate([cos_table, -sin_table], 1), jnp.concatenate([sin_table, cos_table], 1)], 0
    )
    return (cos_table, sin_table, right_forward, right_inverse)


def swap_halves(values):
    half_width = values.shape[-1] // 2
    return jnp.concatenate([-values[..., half_width:], values[..., :half_width]], -1)


def left_product(table, values):
    return jnp.einsum("ja,...am->...jm", table, values, preferred_element_type=jnp.float32)


def forward_transform(sub_grid, tables):
    cos_table, sin_table, right_forward, right_inverse = tables
    half = (
        left_product(cos_table, sub_grid) + left_product(sin_table, swap_halves(sub_grid))
    ).astype(jnp.bfloat16)
    return jnp.einsum(
        "...jb,bm->...jm", half, right_forward, preferred_element_type=jnp.float32
    ).astype(jnp.bfloat16)


def inverse_transform(sub_grid, tables):
    cos_table, sin_table, right_forward, right_inverse = tables
    half = (
        left_product(cos_table, sub_grid) - left_product(sin_table, swap_halves(sub_grid))
    ).astype(jnp.bfloat16)
    return jnp.einsum(
        "...jb,bm->...jm", half, right_inverse, preferred_element_type=jnp.float32
    ).astype(jnp.bfloat16)


def kernels(coords):
    pixel_grid = jnp.arange(SUB, dtype=jnp.int32).astype(jnp.float32)
    delta_u = pixel_grid[None, None, :] - coords[:, 0, :, None]
    delta_v = pixel_grid[None, None, :] - coords[:, 1, :, None]
    return (jnp.exp(-KERNEL_COEF * delta_u * delta_u), jnp.exp(-KERNEL_COEF * delta_v * delta_v))


def pick_windows(model_local, meta_flat):
    slot_total = meta_flat.shape[0]
    zero_index = jnp.zeros((), jnp.int32)

    def pick_one(slot, buffer):
        row_start = meta_flat[slot, 0].astype(jnp.int32)
        col_start = meta_flat[slot, 1].astype(jnp.int32)
        window = lax.dynamic_slice(model_local, (row_start, zero_index, col_start), (SUB, 2, SUB))
        window = window.reshape(1, SUB, 2 * SUB)
        return lax.dynamic_update_slice(
            buffer, window, (slot.astype(jnp.int32), zero_index, zero_index)
        )

    start_buffer = jnp.zeros((slot_total, SUB, 2 * SUB), model_local.dtype)
    return lax.fori_loop(0, slot_total, pick_one, start_buffer)


def add_windows(values_flat, meta_flat):
    slot_total = meta_flat.shape[0]
    zero_index = jnp.zeros((), jnp.int32)

    def add_one(slot, canvas):
        row_start = meta_flat[slot, 0].astype(jnp.int32)
        col_start = meta_flat[slot, 1].astype(jnp.int32)
        corner = (row_start, zero_index, col_start)
        window = lax.dynamic_slice(canvas, corner, (SUB, 2, SUB))
        return lax.dynamic_update_slice(canvas, window + values_flat[slot], corner)

    start_canvas = jnp.zeros((F_ROWS, 2, FACET), jnp.float32)
    return lax.fori_loop(0, slot_total, add_one, start_canvas)


def per_device(
    visibility, uv_coords, vis_count, subgrid_facet, row_offset, col_offset, model_facet
):
    facet_count = lax.axis_size("facet")
    subgrid_local = visibility.shape[0]
    capacity = max(2, 2 * subgrid_local // facet_count)
    tables = dft_tables(SUB)
    kernel_u, kernel_v = kernels(uv_coords)
    live_mask = (jnp.arange(NV, dtype=jnp.int32)[None, :] < vis_count[:, None]).astype(jnp.float32)
    weighted = visibility * live_mask[:, None, :]
    spread = (
        (jnp.transpose(weighted, (0, 2, 1))[:, :, :, None] * kernel_v[:, :, None, :])
        .reshape(subgrid_local, NV, 2 * SUB)
        .astype(jnp.bfloat16)
    )
    kernel_low = kernel_u.astype(jnp.bfloat16)
    gridded = jnp.einsum(
        "ska,skm->sam", kernel_low, spread, preferred_element_type=jnp.float32
    ).astype(jnp.bfloat16)
    facet_ids = subgrid_facet[:, 0]
    one_hot = (facet_ids[:, None] == jnp.arange(facet_count, dtype=jnp.int32)[None, :]).astype(
        jnp.int32
    )
    slot_index = jnp.sum(one_hot * jnp.cumsum(one_hot, 0), 1) - 1
    send_grid = (
        jnp.zeros((facet_count, capacity, SUB, 2 * SUB), jnp.bfloat16)
        .at[facet_ids, slot_index]
        .set(gridded)
    )
    meta_rows = jnp.stack([row_offset, col_offset, jnp.ones_like(row_offset)], 1)
    slot_meta = (
        jnp.zeros((facet_count, capacity, 3), jnp.int32).at[facet_ids, slot_index].set(meta_rows)
    )
    model_local = model_facet[0]
    incoming = lax.all_to_all(send_grid, "facet", split_axis=0, concat_axis=0, tiled=True)
    meta_in = lax.all_to_all(slot_meta, "facet", split_axis=0, concat_axis=0, tiled=True)
    patch = forward_transform(incoming, tables)
    lead_shape = meta_in.shape[:-1]
    meta_flat = meta_in.reshape(-1, 3)
    picked = pick_windows(model_local, meta_flat).reshape(lead_shape + (SUB, 2 * SUB))
    going_back = inverse_transform(picked, tables)
    returned = lax.all_to_all(going_back, "facet", split_axis=0, concat_axis=0, tiled=True)
    patches, meta_back, returned = (patch, meta_in, returned)
    valid = meta_back[..., 2].astype(jnp.float32)
    values = patches.astype(jnp.float32) * valid[..., None, None]
    values_flat = values.reshape(-1, SUB, 2, SUB)
    canvas = add_windows(values_flat, meta_back.reshape(-1, 3))
    share = lax.psum_scatter(
        canvas.astype(jnp.bfloat16), "chan", scatter_dimension=0, tiled=True
    ).astype(jnp.float32)
    facet_image = share[None]
    model_back = returned[facet_ids, slot_index]
    degridded = jnp.einsum(
        "ska,sam->skm", kernel_low, model_back, preferred_element_type=jnp.float32
    ).reshape(subgrid_local, NV, 2, SUB)
    predicted = jnp.sum(degridded * kernel_v[:, :, None, :], -1)
    residual_vis = (visibility - jnp.transpose(predicted, (0, 2, 1))) * live_mask[:, None, :]
    return (facet_image, residual_vis)


def solution(mesh):
    in_specs = (
        P(("facet", "chan"), None, None),
        P(("facet", "chan"), None, None),
        P(("facet", "chan")),
        P(("facet", "chan"), None),
        P(("facet", "chan")),
        P(("facet", "chan")),
        P("facet", None, None, None),
    )
    out_specs = (P("facet", "chan", None, None), P(("facet", "chan"), None, None))
    return jax.shard_map(
        per_device, mesh=mesh, in_specs=in_specs, out_specs=out_specs, check_vma=False
    )
```

profile of v0, /device:TPU:2, one launch (start us, length us, event | category | flops | bytes accessed | tf_op | source)
XLA Modules:
  0.0 887.9 jit_solution(2881102065058775351)
XLA Ops:
  10.8 2.2 scatter_fusion
  13.0 7.5 all-to-all-start
  22.6 4.2 all-to-all-done
  26.8 169.3 %while.27 = (s32[]{:T(128)}, bf16[32,64,128]{2,1,0:T(8,128)(2,1)S(1)}, s32[32,3]{0,1:T(4,128)S(1)}, bf16[128,2,4096]{2,1,0:T(2,128)(2,1)}, s32[]{:T(128)}, /*index=5*/s32[]{:T(128)}, s32[]{:T(128)}, s32[]{:T(128)}) while((s32[]{:T(128)}, bf16[32,64,128]{2,1,0:T(8,128)(2,1)S(1)}, s32[32,3]{0,1:T(4,128)S(1)}, bf16[128,2,4096]{2,1,0:T(2,128)(2,1)}, ...), condition=%wide.region_8.9_spmd, body=%wide.region_7.8_spmd.sunk | while | flops 8 | bytes 98497 | solution.py:82
  198.2 4.8 all-to-all-start.2
  203.5 7.7 all-to-all-done.2
  214.9 2.6 scatter_fusion.1
  217.6 5.8 all-to-all-start.1
  223.8 7.4 all-to-all-done.1
  233.7 4.0 broadcast_in_dim.13
  237.7 331.3 %while.26 = (s32[]{:T(128)}, f32[128,2,4096]{2,1,0:T(2,128)}, s32[32,3]{0,1:T(4,128)S(1)}, f32[32,64,2,64]{3,2,1,0:T(2,128)S(1)}, s32[]{:T(128)}, /*index=5*/s32[]{:T(128)}, s32[]{:T(128)}, s32[]{:T(128)}) while((s32[]{:T(128)}, f32[128,2,4096]{2,1,0:T(2,128)}, s32[32,3]{0,1:T(4,128)S(1)}, f32[32,64,2,64]{3,2,1,0:T(2,128)S(1)}, s32[]{:T(128)}, ...), condition=%wide.region_5.6_spmd, body=%wide.region_4.5_spmd.sunk | while | flops 8200 | bytes 164037 | solution.py:97
  243.1 10.9 %dynamic_update_slice.17 = f32[128,2,4096]{2,1,0:T(2,128)} dynamic-update-slice(f32[128,2,4096]{2,1,0:T(2,128)} %get-tuple-element.285, f32[64,2,64]{2,1,0:T(2,128)S(1)} %bitcast_add_fusion.2, s32[]{:T(128)S(6)} %select_n.127, s32[]{:T(128)} %constant.105.clone.1..sunk, s32[]{:T(128)S(6)} %select_n.128) | dynamic-update-slice | bytes 65540 | tf_op jit(solution)/shard_map/while/body/eval_jaxpr/dynamic_update_slice | solution.py:94
  259.4 2.2 dynamic_update_slice.17
  267.1 10.8 %dynamic_update_slice.17 = f32[128,2,4096]{2,1,0:T(2,128)} dynamic-update-slice(f32[128,2,4096]{2,1,0:T(2,128)} %get-tuple-element.285, f32[64,2,64]{2,1,0:T(2,128)S(1)} %bitcast_add_fusion.2, s32[]{:T(128)S(6)} %select_n.127, s32[]{:T(128)} %constant.105.clone.1..sunk, s32[]{:T(128)S(6)} %select_n.128) | dynamic-update-slice | bytes 65540 | tf_op jit(solution)/shard_map/while/body/eval_jaxpr/dynamic_update_slice | solution.py:94
  283.4 2.2 dynamic_update_slice.17
  298.7 2.2 dynamic_update_slice.17
  306.3 2.2 dynamic_update_slice.17
  314.0 2.2 dynamic_update_slice.17
  321.6 10.8 %dynamic_update_slice.17 = f32[128,2,4096]{2,1,0:T(2,128)} dynamic-update-slice(f32[128,2,4096]{2,1,0:T(2,128)} %get-tuple-element.285, f32[64,2,64]{2,1,0:T(2,128)S(1)} %bitcast_add_fusion.2, s32[]{:T(128)S(6)} %select_n.127, s32[]{:T(128)} %constant.105.clone.1..sunk, s32[]{:T(128)S(6)} %select_n.128) | dynamic-update-slice | bytes 65540 | tf_op jit(solution)/shard_map/while/body/eval_jaxpr/dynamic_update_slice | solution.py:94
  337.9 2.2 dynamic_update_slice.17
  345.6 10.9 %dynamic_update_slice.17 = f32[128,2,4096]{2,1,0:T(2,128)} dynamic-update-slice(f32[128,2,4096]{2,1,0:T(2,128)} %get-tuple-element.285, f32[64,2,64]{2,1,0:T(2,128)S(1)} %bitcast_add_fusion.2, s32[]{:T(128)S(6)} %select_n.127, s32[]{:T(128)} %constant.105.clone.1..sunk, s32[]{:T(128)S(6)} %select_n.128) | dynamic-update-slice | bytes 65540 | tf_op jit(solution)/shard_map/while/body/eval_jaxpr/dynamic_update_slice | solution.py:94
  361.9 2.2 dynamic_update_slice.17
  369.5 10.9 %dynamic_update_slice.17 = f32[128,2,4096]{2,1,0:T(2,128)} dynamic-update-slice(f32[128,2,4096]{2,1,0:T(2,128)} %get-tuple-element.285, f32[64,2,64]{2,1,0:T(2,128)S(1)} %bitcast_add_fusion.2, s32[]{:T(128)S(6)} %select_n.127, s32[]{:T(128)} %constant.105.clone.1..sunk, s32[]{:T(128)S(6)} %select_n.128) | dynamic-update-slice | bytes 65540 | tf_op jit(solution)/shard_map/while/body/eval_jaxpr/dynamic_update_slice | solution.py:94
  385.8 2.2 dynamic_update_slice.17
  393.5 2.2 dynamic_update_slice.17
  424.1 10.8 %dynamic_update_slice.17 = f32[128,2,4096]{2,1,0:T(2,128)} dynamic-update-slice(f32[128,2,4096]{2,1,0:T(2,128)} %get-tuple-element.285, f32[64,2,64]{2,1,0:T(2,128)S(1)} %bitcast_add_fusion.2, s32[]{:T(128)S(6)} %select_n.127, s32[]{:T(128)} %constant.105.clone.1..sunk, s32[]{:T(128)S(6)} %select_n.128) | dynamic-update-slice | bytes 65540 | tf_op jit(solution)/shard_map/while/body/eval_jaxpr/dynamic_update_slice | solution.py:94
  448.0 10.9 %dynamic_update_slice.17 = f32[128,2,4096]{2,1,0:T(2,128)} dynamic-update-slice(f32[128,2,4096]{2,1,0:T(2,128)} %get-tuple-element.285, f32[64,2,64]{2,1,0:T(2,128)S(1)} %bitcast_add_fusion.2, s32[]{:T(128)S(6)} %select_n.127, s32[]{:T(128)} %constant.105.clone.1..sunk, s32[]{:T(128)S(6)} %select_n.128) | dynamic-update-slice | bytes 65540 | tf_op jit(solution)/shard_map/while/body/eval_jaxpr/dynamic_update_slice | solution.py:94
  472.0 10.9 %dynamic_update_slice.17 = f32[128,2,4096]{2,1,0:T(2,128)} dynamic-update-slice(f32[128,2,4096]{2,1,0:T(2,128)} %get-tuple-element.285, f32[64,2,64]{2,1,0:T(2,128)S(1)} %bitcast_add_fusion.2, s32[]{:T(128)S(6)} %select_n.127, s32[]{:T(128)} %constant.105.clone.1..sunk, s32[]{:T(128)S(6)} %select_n.128) | dynamic-update-slice | bytes 65540 | tf_op jit(solution)/shard_map/while/body/eval_jaxpr/dynamic_update_slice | solution.py:94
  511.2 10.8 %dynamic_update_slice.17 = f32[128,2,4096]{2,1,0:T(2,128)} dynamic-update-slice(f32[128,2,4096]{2,1,0:T(2,128)} %get-tuple-element.285, f32[64,2,64]{2,1,0:T(2,128)S(1)} %bitcast_add_fusion.2, s32[]{:T(128)S(6)} %select_n.127, s32[]{:T(128)} %constant.105.clone.1..sunk, s32[]{:T(128)S(6)} %select_n.128) | dynamic-update-slice | bytes 65540 | tf_op jit(solution)/shard_map/while/body/eval_jaxpr/dynamic_update_slice | solution.py:94
  535.2 10.9 %dynamic_update_slice.17 = f32[128,2,4096]{2,1,0:T(2,128)} dynamic-update-slice(f32[128,2,4096]{2,1,0:T(2,128)} %get-tuple-element.285, f32[64,2,64]{2,1,0:T(2,128)S(1)} %bitcast_add_fusion.2, s32[]{:T(128)S(6)} %select_n.127, s32[]{:T(128)} %constant.105.clone.1..sunk, s32[]{:T(128)S(6)} %select_n.128) | dynamic-update-slice | bytes 65540 | tf_op jit(solution)/shard_map/while/body/eval_jaxpr/dynamic_update_slice | solution.py:94
  569.0 5.5 convert_element_type.133
  577.1 302.2 %all-reduce.3.cloned.1.call-done = bf16[128,2,4096]{2,1,0:T(2,128)(2,1)} async-done(((bf16[128,2,4096]{2,1,0:T(2,128)(2,1)}), bf16[128,2,4096]{2,1,0:T(2,128)(2,1)}) %all-reduce.3.cloned.1.call-update) | async-done | bytes 2097168
  (248 shorter events, 153.2 us)
Async XLA Ops:
  13.0 13.7 %all-to-all-start = ((s32[16,2,3]{2,1,0:T(2,128)}), s32[16,2,3]{2,1,0:T(2,128)S(1)}, u32[]{:S(2)}, u32[]{:S(2)}) async-start(s32[16,2,3]{2,1,0:T(2,128)} %scatter_fusion), calls=%async_computation | async-start | bytes 32768 | tf_op jit(solution)/shard_map/all_to_all | solution.py:135
  196.7 6.3 copy-start
  198.2 13.0 %all-to-all-start.2 = ((bf16[16,2,64,128]{3,2,1,0:T(8,128)(2,1)}), bf16[16,2,64,128]{3,2,1,0:T(8,128)(2,1)S(1)}, u32[]{:S(2)}, u32[]{:S(2)}) async-start(bf16[16,2,64,128]{3,2,1,0:T(8,128)(2,1)} %convolution_convert_fusion), calls=%async_computation.2 | async-start | bytes 1048576 | tf_op jit(solution)/shard_map/all_to_all | solution.py:141
  217.6 13.6 %all-to-all-start.1 = ((bf16[16,2,64,128]{3,2,1,0:T(8,128)(2,1)}), bf16[16,2,64,128]{3,2,1,0:T(8,128)(2,1)S(1)}, u32[]{:S(2)}, u32[]{:S(2)}) async-start(bf16[16,2,64,128]{3,2,1,0:T(8,128)(2,1)} %scatter_fusion.1), calls=%async_computation.1 | async-start | bytes 1048576 | tf_op jit(solution)/shard_map/all_to_all | solution.py:134
  223.3 656.0 %all-reduce.3.cloned.1.call-start = ((), (), s32[]{:S(2)}) async-start(), calls=%async_computation.3 | async-start | bytes 4194304
  574.5 0.7 copy-start.1
Sparse Core Ops, SparseCore 0:
  574.6 304.6 all-reduce.2
where the time goes:
time: 896 us; the launch traced here: 888 us
  waiting for transfers between devices  321 us (36%)
  local copies, waits for them, and re-layouts  245 us (27%)
  loops' own time  237 us (26%)
  other arithmetic  46.3 us (5%)
  starting transfers between devices  18.3 us (2%)
  between operations  14.8 us (2%)
    unnamed x2, waiting for transfers between devices  302 us
    dynamic_update_slice x32, local copies, waits for them, and re-layouts, add_one(): return lax.dynamic_update_slice(canvas, window + values_flat[slot], corner)  157 us
    another operation x1, loops' own time, add_windows(): return lax.fori_loop(0, slot_total, add_one, start_canvas)  121 us
    another operation x1, loops' own time, pick_windows(): return lax.fori_loop(0, slot_total, pick_one, start_buffer)  117 us
    add x32, other arithmetic, add_one(): return lax.dynamic_update_slice(canvas, window + values_flat[slot], corner)  33.5 us
    dynamic_slice x32, local copies, waits for them, and re-layouts, pick_one(): lax.dynamic_slice(model_local, (row_start, zero_index, col_start), (SUB,...  30.5 us
    dynamic_slice x32, local copies, waits for them, and re-layouts, add_one(): col_start = meta_flat[slot, 1].astype(jnp.int32)  19.7 us
    dynamic_slice x32, local copies, waits for them, and re-layouts, pick_one(): col_start = meta_flat[slot, 1].astype(jnp.int32)  18.8 us
  transfers between devices with their start and end apart: 4, of which 4 were waited for; matrix products, arithmetic and copies ran while one was open for 0% of the time, Pallas kernels for 0%

commit v1 on v0

v1 whole, which is shorter than its diff:
```python
import functools
import math

import jax
import jax.numpy as jnp
import numpy as np
from jax import lax
from jax.experimental import pallas as pl
from jax.experimental.pallas import tpu as pltpu
from jax.sharding import PartitionSpec as P

SUB = 64
FACET = 4096
F_ROWS = 128
NV = 512
LANES = 128
TILES = FACET // LANES
SLOTS = 2


def dft_tables():
    line = np.arange(SUB)
    angle = 2.0 * math.pi * (line[:, None] * line[None, :] % SUB) / SUB
    cos_table = (np.cos(angle) / math.sqrt(SUB)).astype(jnp.bfloat16)
    sin_table = (-np.sin(angle) / math.sqrt(SUB)).astype(jnp.bfloat16)
    left_forward = np.concatenate([cos_table, sin_table], 1)
    left_inverse = np.concatenate([cos_table, -sin_table], 1)
    right_forward = np.concatenate(
        [np.concatenate([cos_table, sin_table], 1), np.concatenate([-sin_table, cos_table], 1)], 0
    )
    right_inverse = np.concatenate(
        [np.concatenate([cos_table, -sin_table], 1), np.concatenate([sin_table, cos_table], 1)], 0
    )
    return left_forward, right_forward, left_inverse, right_inverse


def kernel_of(coords):
    pixels = lax.broadcasted_iota(jnp.int32, (SUB, NV), 0).astype(jnp.float32)
    delta = pixels - coords
    return jnp.exp(-(delta * delta))


def live_row(count):
    lane = lax.broadcasted_iota(jnp.int32, (1, NV), 1)
    return (lane < count).astype(jnp.float32)


def facet_peers(me, side):
    x, y = me // side, lax.rem(me, side)
    order = {0: 0, 2: 2}
    steps = [(dx, dy) for dx in range(side) for dy in range(side) if dx or dy]
    steps.sort(key=lambda step: -sum(min(d, side - d) for d in step))
    return [lax.rem(x + dx, side) * side + lax.rem(y + dy, side) for dx, dy in steps], [
        lax.rem(x + side - dx, side) * side + lax.rem(y + side - dy, side) for dx, dy in steps
    ]


def grid_kernel(
    facets, side, subgrids,
    cnt, fid, row, col, vis, uv,
    ku_out, kv_out, grid_in, meta_in,
    grids, grid_send, meta_send, first, last,
    send_sem, recv_sem, meta_send_sem, meta_recv_sem, own_sem,
):
    me = lax.axis_index("facet")
    targets, sources = facet_peers(me, side)
    barrier = pltpu.get_barrier_semaphore()
    for peer in targets:
        pl.semaphore_signal(barrier, inc=1, device_id={"facet": peer})

    ids = [fid[s] for s in range(subgrids)]

    def find(facet, carry):
        low = jnp.int32(subgrids)
        high = jnp.int32(-1)
        for s in range(subgrids):
            same = ids[s] == facet
            high = jnp.where(same, s, high)
            back = subgrids - 1 - s
            low = jnp.where(ids[back] == facet, back, low)
        first[facet] = low
        last[facet] = high
        return carry

    lax.fori_loop(0, facets, find, 0)

    def grid_one(s, carry):
        ku = kernel_of(uv[s, pl.ds(0, 1), :]).astype(jnp.bfloat16)
        kv = kernel_of(uv[s, pl.ds(1, 1), :])
        live = live_row(cnt[s])
        re = (vis[s, pl.ds(0, 1), :] * live) * kv
        im = (vis[s, pl.ds(1, 1), :] * live) * kv
        spread = jnp.concatenate([re.astype(jnp.bfloat16), im.astype(jnp.bfloat16)], 0)
        ku_out[s] = ku
        kv_out[s] = kv.astype(jnp.bfloat16)
        grids[s] = lax.dot_general(
            ku, spread, (((1,), (1,)), ((), ())), preferred_element_type=jnp.float32
        ).astype(jnp.bfloat16)
        return carry

    lax.fori_loop(0, subgrids, grid_one, 0, unroll=2)

    lane = lax.broadcasted_iota(jnp.int32, (1, LANES), 1)

    def pack(facet, carry):
        low, high = first[facet], last[facet]
        one = jnp.minimum(low, subgrids - 1)
        two = jnp.maximum(high, 0)
        grid_send[facet, 0] = grids[one]
        grid_send[facet, 1] = grids[two]
        values = (
            (high >= 0).astype(jnp.int32), row[one], col[one],
            (high > low).astype(jnp.int32), row[two], col[two],
        )
        line = jnp.zeros((1, LANES), jnp.int32)
        for place, value in enumerate(values):
            line = jnp.where(lane == place, value, line)
        meta_send[facet] = line
        return carry

    lax.fori_loop(0, facets, pack, 0)

    pl.semaphore_wait(barrier, facets - 1)
    started = []
    for i, peer in enumerate(targets):
        for src, dst, ssem, rsem in (
            (meta_send, meta_in, meta_send_sem, meta_recv_sem),
            (grid_send, grid_in, send_sem, recv_sem),
        ):
            copy = pltpu.make_async_remote_copy(
                src_ref=src.at[peer], dst_ref=dst.at[me], send_sem=ssem.at[i], recv_sem=rsem.at[i],
                device_id={"facet": peer},
            )
            copy.start()
            started.append(copy)
    own = pltpu.make_async_copy(grid_send.at[me], grid_in.at[me], own_sem.at[0])
    own_meta = pltpu.make_async_copy(meta_send.at[me], meta_in.at[me], own_sem.at[1])
    own.start()
    own_meta.start()
    for copy in started:
        copy.wait()
    own.wait()
    own_meta.wait()


def swapped(values):
    half = values.shape[-1] // 2
    return jnp.concatenate([-values[:, half:], values[:, :half]], 1)


def left_pair(table, one, two):
    upper = jnp.concatenate([one, two], 1)
    lower = jnp.concatenate([swapped(one), swapped(two)], 1)
    out = jnp.dot(table, jnp.concatenate([upper, lower], 0), preferred_element_type=jnp.float32)
    return out.astype(jnp.bfloat16)


def facet_kernel(
    facets, chans,
    meta, grid_in, model, left_f, right_f, left_i, right_i,
    canvas_out, back_out,
    canvas, halves, patches,
):
    rows = F_ROWS // chans
    lane = lax.broadcasted_iota(jnp.int32, (SUB, LANES), 1)
    zero = jnp.zeros((F_ROWS, LANES), jnp.float32)

    def clear(tile, carry):
        canvas[0, tile] = zero
        canvas[1, tile] = zero
        return carry

    lax.fori_loop(0, TILES + 1, clear, 0)

    def forward(facet, carry):
        out = left_pair(left_f[...], grid_in[facet, 0], grid_in[facet, 1])
        halves[pl.ds(pl.multiple_of(facet * 2 * SUB, 2 * SUB), SUB), :] = out[:, :LANES]
        halves[pl.ds(pl.multiple_of(facet * 2 * SUB + SUB, SUB), SUB), :] = out[:, LANES:]
        return carry

    lax.fori_loop(0, facets, forward, 0, unroll=4)

    def forward_right(block, carry):
        at = pl.ds(pl.multiple_of(block * 256, 256), 256)
        patches[at, :] = jnp.dot(halves[at, :], right_f[...], preferred_element_type=jnp.float32)
        return carry

    lax.fori_loop(0, facets * SLOTS * SUB // 256, forward_right, 0, unroll=2)

    def add(facet, carry):
        for slot in range(SLOTS):
            valid = meta[facet, 0, 3 * slot]

            @pl.when(valid > 0)
            def _():
                top = meta[facet, 0, 3 * slot + 1]
                col = meta[facet, 0, 3 * slot + 2]
                tile, shift = col // LANES, lax.rem(col, LANES)
                patch = patches[pl.ds(pl.multiple_of((facet * 2 + slot) * SUB, SUB), SUB), :]
                inside = (lane >= shift) & (lane < shift + SUB)
                at = pl.ds(top, SUB)
                turned = (
                    pltpu.roll(patch, shift, 1),
                    pltpu.roll(patch, lax.rem(shift + SUB, LANES), 1),
                )
                for part in range(2):
                    canvas[part, tile, at, :] += jnp.where(inside, turned[part], 0.0)

                @pl.when(shift > SUB)
                def _():
                    beyond = lane < shift - SUB
                    for part in range(2):
                        canvas[part, tile + 1, at, :] += jnp.where(beyond, turned[part], 0.0)

        return carry

    lax.fori_loop(0, facets, add, 0)

    def emit(pair, carry):
        for part in range(2):
            for chan in range(chans):
                both = jnp.concatenate(
                    [canvas[part, 2 * pair + i, pl.ds(chan * rows, rows), :] for i in range(2)], 0
                )
                at = pl.ds(pl.multiple_of(part * (TILES * rows) + pair * 2 * rows, 2 * rows), 2 * rows)
                canvas_out[chan, at, :] = both.astype(jnp.bfloat16)
        return carry

    lax.fori_loop(0, TILES // 2, emit, 0)

    def pick(facet, carry):
        picked = []
        for slot in range(SLOTS):
            top = meta[facet, 0, 3 * slot + 1]
            col = meta[facet, 0, 3 * slot + 2]
            tile, shift = col // LANES, lax.rem(col, LANES)
            after = jnp.minimum(tile + 1, TILES - 1)
            at = pl.ds(top, SUB)
            parts = [
                jnp.where(lane >= shift, model[part, tile, at, :], model[part, after, at, :])
                for part in range(2)
            ]
            re = pltpu.roll(parts[0], lax.rem(LANES - shift, LANES), 1)
            im = pltpu.roll(parts[1], lax.rem(LANES + SUB - shift, LANES), 1)
            picked.append(jnp.where(lane < SUB, re, im).astype(jnp.bfloat16))
        out = left_pair(left_i[...], picked[0], picked[1])
        halves[pl.ds(pl.multiple_of(facet * 2 * SUB, 2 * SUB), SUB), :] = out[:, :LANES]
        halves[pl.ds(pl.multiple_of(facet * 2 * SUB + SUB, SUB), SUB), :] = out[:, LANES:]
        return carry

    lax.fori_loop(0, facets, pick, 0, unroll=2)

    def inverse_right(block, carry):
        at = pl.ds(pl.multiple_of(block * 256, 256), 256)
        out = jnp.dot(halves[at, :], right_i[...], preferred_element_type=jnp.float32)
        out = out.astype(jnp.bfloat16)
        for i in range(2):
            for slot in range(SLOTS):
                begin = (2 * i + slot) * SUB
                back_out[2 * block + i, slot] = out[begin : begin + SUB]
        return carry

    lax.fori_loop(0, facets * SLOTS * SUB // 256, inverse_right, 0, unroll=2)


PIECES = 4


def exchange_kernel(
    facets, side, chans,
    canvas, back,
    total, returned,
    pair_buf, send_buf, recv_buf,
    pair_send, pair_recv, ring_send, ring_recv, back_send, back_recv, own_sem,
):
    chips = chans // 2
    me_f, me_c = lax.axis_index("facet"), lax.axis_index("chan")
    z, core = me_c // 2, lax.rem(me_c, 2)
    partner = z * 2 + 1 - core
    right = lax.rem(z + 1, chips) * 2 + core
    left = lax.rem(z + chips - 1, chips) * 2 + core
    targets, _ = facet_peers(me_f, side)
    barrier = pltpu.get_barrier_semaphore()
    for peer in (partner, right, left):
        pl.semaphore_signal(barrier, inc=1, device_id={"chan": peer})
    for peer in targets:
        pl.semaphore_signal(barrier, inc=1, device_id={"facet": peer})
    pl.semaphore_wait(barrier, 3 + facets - 1)

    half = chips // 2
    offsets = [half]
    for d in range(half - 1, 0, -1):
        offsets += [d, chips - d]
    offsets += [0]
    waits = []
    pair_copy = {}
    for offset in offsets:
        there = lax.rem(z + offset, chips)
        copy = pltpu.make_async_remote_copy(
            src_ref=canvas.at[2 * there + 1 - core], dst_ref=pair_buf.at[offset],
            send_sem=pair_send.at[offset], recv_sem=pair_recv.at[offset], device_id={"chan": partner},
        )
        copy.start()
        pair_copy[offset] = copy
    for i, peer in enumerate(targets):
        copy = pltpu.make_async_remote_copy(
            src_ref=back.at[peer], dst_ref=returned.at[me_f],
            send_sem=back_send.at[i], recv_sem=back_recv.at[i], device_id={"facet": peer},
        )
        copy.start()
        waits.append(copy)
    own = pltpu.make_async_copy(back.at[me_f], returned.at[me_f], own_sem)
    own.start()

    depth = canvas.shape[1] // PIECES
    arrived = set()

    def mine(offset, piece):
        if offset not in arrived:
            arrived.add(offset)
            pair_copy[offset].wait_recv()
        at = pl.ds(piece * depth, depth)
        there = lax.rem(z + offset, chips)
        return canvas[2 * there + core, at, :].astype(jnp.float32) + pair_buf[offset, at, :].astype(
            jnp.float32
        )

    def length(piece, way):
        return half - (piece + way) % 2

    ring = {}
    for step in range(half + 1):
        for piece in range(PIECES):
            for way in range(2):
                count = length(piece, way)
                if step >= count:
                    continue
                distance = count - step
                offset = distance if way == 0 else chips - distance
                value = mine(offset % chips, piece)
                slot = (way * PIECES + piece) * half + step
                if step > 0:
                    ring[way, piece, step - 1].wait_recv()
                    value = value + recv_buf[slot - 1].astype(jnp.float32)
                send_buf[slot] = value.astype(jnp.bfloat16)
                copy = pltpu.make_async_remote_copy(
                    src_ref=send_buf.at[slot], dst_ref=recv_buf.at[slot],
                    send_sem=ring_send.at[slot], recv_sem=ring_recv.at[slot],
                    device_id={"chan": right if way == 0 else left},
                )
                copy.start()
                ring[way, piece, step] = copy
    for piece in range(PIECES):
        value = mine(0, piece)
        for way in range(2):
            step = length(piece, way) - 1
            ring[way, piece, step].wait_recv()
            value = value + recv_buf[(way * PIECES + piece) * half + step].astype(jnp.float32)
        total[pl.ds(piece * depth, depth), :] = value
    for copy in pair_copy.values():
        copy.wait_send()
    for copy in ring.values():
        copy.wait_send()
    for copy in waits:
        copy.wait()
    own.wait()


def residual_kernel(subgrids, facets, cnt, fid, vis, ku, kv, returned, out, seen):
    def clear(facet, carry):
        seen[facet] = 0
        return carry

    lax.fori_loop(0, facets, clear, 0)

    def one(s, carry):
        facet = fid[s]
        slot = seen[facet]
        seen[facet] = slot + 1
        image = returned[facet, slot]
        inner = lax.dot_general(
            image, ku[s], (((0,), (0,)), ((), ())), preferred_element_type=jnp.float32
        )
        weight = kv[s].astype(jnp.float32)
        live = live_row(cnt[s])
        for part in range(2):
            predicted = jnp.sum(inner[part * SUB : (part + 1) * SUB] * weight, 0, keepdims=True)
            out[s, pl.ds(part, 1), :] = (vis[s, pl.ds(part, 1), :] - predicted) * live
        return carry

    lax.fori_loop(0, subgrids, one, 0)


VMEM = pl.BlockSpec(memory_space=pltpu.VMEM)
SMEM = pl.BlockSpec(memory_space=pltpu.SMEM)


def per_device(
    visibility, uv_coords, vis_count, subgrid_facet, row_offset, col_offset, model_facet
):
    facets, chans = lax.axis_size("facet"), lax.axis_size("chan")
    side = math.isqrt(facets)
    chips = chans // 2
    subgrids = visibility.shape[0]
    rows = F_ROWS // chans
    shape = jax.ShapeDtypeStruct
    left_f, right_f, left_i, right_i = (jnp.asarray(table) for table in dft_tables())
    ids = subgrid_facet[:, 0]
    big = 60 << 20

    ku, kv, grid_in, meta = pl.pallas_call(
        functools.partial(grid_kernel, facets, side, subgrids),
        out_shape=(
            shape((subgrids, SUB, NV), jnp.bfloat16),
            shape((subgrids, SUB, NV), jnp.bfloat16),
            shape((facets, SLOTS, SUB, LANES), jnp.bfloat16),
            shape((facets, 1, LANES), jnp.int32),
        ),
        in_specs=[SMEM] * 4 + [VMEM] * 2,
        out_specs=(VMEM,) * 4,
        scratch_shapes=[
            pltpu.VMEM((subgrids, SUB, LANES), jnp.bfloat16),
            pltpu.VMEM((facets, SLOTS, SUB, LANES), jnp.bfloat16),
            pltpu.VMEM((facets, 1, LANES), jnp.int32),
            pltpu.SMEM((facets,), jnp.int32),
            pltpu.SMEM((facets,), jnp.int32),
            pltpu.SemaphoreType.DMA((facets - 1,)),
            pltpu.SemaphoreType.DMA((facets - 1,)),
            pltpu.SemaphoreType.DMA((facets - 1,)),
            pltpu.SemaphoreType.DMA((facets - 1,)),
            pltpu.SemaphoreType.DMA((2,)),
        ],
        compiler_params=pltpu.CompilerParams(collective_id=0, has_side_effects=True),
        name="grid_and_send",
    )(vis_count, ids, row_offset, col_offset, visibility, uv_coords)

    model = (
        model_facet[0]
        .reshape(F_ROWS, 2, TILES, LANES)
        .transpose(1, 2, 0, 3)
        .astype(jnp.float32)
    )
    canvas, back = pl.pallas_call(
        functools.partial(facet_kernel, facets, chans),
        out_shape=(
            shape((chans, 2 * TILES * rows, LANES), jnp.bfloat16),
            shape((facets, SLOTS, SUB, LANES), jnp.bfloat16),
        ),
        in_specs=[SMEM] + [VMEM] * 6,
        out_specs=(VMEM,) * 2,
        scratch_shapes=[
            pltpu.VMEM((2, TILES + 1, F_ROWS, LANES), jnp.float32),
            pltpu.VMEM((facets * SLOTS * SUB, LANES), jnp.bfloat16),
            pltpu.VMEM((facets * SLOTS * SUB, LANES), jnp.float32),
        ],
        compiler_params=pltpu.CompilerParams(vmem_limit_bytes=40 << 20),
        name="facet_work",
    )(meta, grid_in, model, left_f, right_f, left_i, right_i)

    depth = 2 * TILES * rows // PIECES
    links = 2 * PIECES * (chips // 2)
    total, returned = pl.pallas_call(
        functools.partial(exchange_kernel, facets, side, chans),
        out_shape=(
            shape((2 * TILES * rows, LANES), jnp.float32),
            shape((facets, SLOTS, SUB, LANES), jnp.bfloat16),
        ),
        in_specs=[VMEM] * 2,
        out_specs=(VMEM,) * 2,
        scratch_shapes=[
            pltpu.VMEM((chips, 2 * TILES * rows, LANES), jnp.bfloat16),
            pltpu.VMEM((links, depth, LANES), jnp.bfloat16),
            pltpu.VMEM((links, depth, LANES), jnp.bfloat16),
            pltpu.SemaphoreType.DMA((chips,)),
            pltpu.SemaphoreType.DMA((chips,)),
            pltpu.SemaphoreType.DMA((links,)),
            pltpu.SemaphoreType.DMA((links,)),
            pltpu.SemaphoreType.DMA((facets - 1,)),
            pltpu.SemaphoreType.DMA((facets - 1,)),
            pltpu.SemaphoreType.DMA,
        ],
        compiler_params=pltpu.CompilerParams(collective_id=1, has_side_effects=True),
        name="reduce_and_return",
    )(canvas, back)

    residual = pl.pallas_call(
        functools.partial(residual_kernel, subgrids, facets),
        out_shape=shape(visibility.shape, jnp.float32),
        in_specs=[SMEM] * 2 + [VMEM] * 4,
        out_specs=VMEM,
        scratch_shapes=[pltpu.SMEM((facets,), jnp.int32)],
        name="residual",
    )(vis_count, ids, visibility, ku, kv, returned)

    image = total.reshape(2, TILES, rows, LANES).transpose(2, 0, 1, 3).reshape(1, rows, 2, FACET)
    return image, residual


def solution(mesh):
    in_specs = (
        P(("facet", "chan"), None, None),
        P(("facet", "chan"), None, None),
        P(("facet", "chan")),
        P(("facet", "chan"), None),
        P(("facet", "chan")),
        P(("facet", "chan")),
        P("facet", None, None, None),
    )
    out_specs = (P("facet", "chan", None, None), P(("facet", "chan"), None, None))
    return jax.shard_map(
        per_device, mesh=mesh, in_specs=in_specs, out_specs=out_specs, check_vma=False
    )
```

time: 896 us -> 74.4 us (0.08)
  waiting for transfers between devices: 321 us -> 0 us
  loops' own time: 237 us -> 0 us
  local copies, waits for them, and re-layouts: 245 us -> 15.1 us
  Pallas kernels: 0 us -> 57.2 us
  other arithmetic: 46.3 us -> 0 us
  starting transfers between devices: 18.3 us -> 0 us
  between operations: 14.8 us -> 0.76 us
    unnamed x2 -> x0, waiting for transfers between devices: 302 us -> none
    another operation x2 -> x0, loops' own time: 237 us -> none  [the longest x1 121 us: add_windows(): return lax.fori_loop(0, slot_total, add_one, start_canvas)]
    dynamic_update_slice x64 -> x0, local copies, waits for them, and re-layouts: 158 us -> none  [the longest x32 157 us: add_one(): return lax.dynamic_update_slice(canvas, window + values_flat[slot], corner)]
    dynamic_slice x96 -> x0, local copies, waits for them, and re-layouts: 69 us -> none  [the longest x32 30.5 us: pick_one(): lax.dynamic_slice(model_local, (row_start, zero_index, col_start), (SUB,...]
    pallas_call x0 -> x4, Pallas kernels: none -> 57.2 us  [the longest x1 27.5 us: per_device(): pl.pallas_call(functools.partial(exchange_kernel, facets, side, chans), o...]
    add x32 -> x0, other arithmetic: 33.5 us -> none  [add_one(): return lax.dynamic_update_slice(canvas, window + values_flat[slot], corner)]
    all_to_all x3 -> x0, waiting for transfers between devices: 19.2 us -> none  [the longest x1 7.66 us: per_device(): lax.all_to_all(going_back, 'facet', split_axis=0, concat_axis=0, tiled=True)]
    all_to_all x3 -> x0, starting transfers between devices: 18.1 us -> none  [the longest x1 7.48 us: per_device(): lax.all_to_all(slot_meta, 'facet', split_axis=0, concat_axis=0, tiled=True)]
  transfers between devices with their start and end apart: 4 -> 0, of which waited for: 4 -> 0; matrix products, arithmetic and copies ran while one was open for 0% -> 0% of each run, Pallas kernels for 0% -> 0%
where the time goes in v1:
time: 74.4 us; the launch traced here: 73 us
  Pallas kernels  57.2 us (77%)
  local copies, waits for them, and re-layouts  15.1 us (20%)
  between operations  0.76 us (1%)
    pallas_call x1, Pallas kernels, per_device(): pl.pallas_call(functools.partial(exchange_kernel, facets, side, chans), o...  27.5 us
    pallas_call x1, Pallas kernels, per_device(): pl.pallas_call(functools.partial(grid_kernel, facets, side, subgrids), ou...  15.4 us
    unnamed x21, local copies, waits for them, and re-layouts  11 us
    pallas_call x1, Pallas kernels, per_device(): pl.pallas_call(functools.partial(facet_kernel, facets, chans), out_shape=...  8 us
    pallas_call x1, Pallas kernels, per_device(): pl.pallas_call(functools.partial(residual_kernel, subgrids, facets), out_...  6.18 us
    convert_element_type x1, local copies, waits for them, and re-layouts, per_device(): model = model_facet[0].reshape(F_ROWS, 2, TILES, LANES).transpose(1, 2, 0...  3.19 us

profile of v1, /device:TPU:2, one launch (start us, length us, event | category | flops | bytes accessed | tf_op | source)
XLA Modules:
  0.0 73.0 jit_solution(13004156888287504649)
XLA Ops:
  0.6 4.9 %copy.14 = bf16[1,128,2,4096]{1,3,2,0:T(8,128)(2,1)S(1)} copy(bf16[1,128,2,4096]{3,2,1,0:T(2,128)(2,1)} %param.17) | data formatting | bytes 4194304 | tf_op args[6]
  5.5 0.0 copy-start.4
  5.5 0.0 copy-start.5
  5.6 0.0 copy-start.6
  5.6 0.0 copy-start.7
  5.6 3.2 %copy.15 = f32[128,2,32,128]{3,0,2,1:T(8,128)} copy(bf16[128,2,32,128]{0,3,2,1:T(8,128)(2,1)S(1)} %bitcast.10) | data formatting | bytes 6291456 | tf_op jit(solution)/shard_map/convert_element_type | solution.py:441
  8.8 15.4 %grid_and_send.1 = (bf16[16,64,512]{2,1,0:T(8,128)(2,1)}, bf16[16,64,512]{2,1,0:T(8,128)(2,1)}, bf16[16,2,64,128]{3,2,1,0:T(8,128)(2,1)}, s32[16,1,128]{2,1,0:T(1,128)}) custom-call(s32[16]{0:T(128)} %cnt.3, s32[16]{0:T(128)} %bitcast.12, s32[16]{0:T(128)} %row.1, s32[16]{0:T(128)} %col.1, f32[16,2,512]{2,1,0:T(2,128)} %vis.3, f32[16,2,512]{2,1,0:T(2,128)} %uv.1), custom_call_target="tpu_custom_call" | custom-call | tf_op jit(solution)/shard_map/grid_and_send/pallas_call | solution.py:411
  24.2 0.0 copy-done.4
  24.2 0.0 copy-done.5
  24.2 0.0 copy-done.6
  24.2 0.0 copy-done.7
  24.3 0.0 copy-start
  24.3 2.2 %copy-done = f32[128,2,32,128]{3,0,2,1:T(8,128)S(1)} copy-done((f32[128,2,32,128]{3,0,2,1:T(8,128)S(1)}, f32[128,2,32,128]{3,0,2,1:T(8,128)}, u32[]{:S(2)}) %copy-start) | copy-done | bytes 4194328
  26.4 0.0 copy-start.2
  26.4 1.0 %copy-done.2 = bf16[16,2,64,128]{3,2,1,0:T(8,128)(2,1)S(1)} copy-done((bf16[16,2,64,128]{3,2,1,0:T(8,128)(2,1)S(1)}, bf16[16,2,64,128]{3,2,1,0:T(8,128)(2,1)}, u32[]{:S(2)}) %copy-start.2) | copy-done | bytes 524312
  27.5 0.0 copy-start.8
  27.5 0.7 copy-done.8
  28.2 8.0 %facet_work.1 = (bf16[16,512,128]{2,1,0:T(8,128)(2,1)S(1)}, bf16[16,2,64,128]{3,2,1,0:T(8,128)(2,1)S(1)}) custom-call(s32[16,1,128]{2,1,0:T(1,128)S(1)} %copy-done.8, bf16[16,2,64,128]{3,2,1,0:T(8,128)(2,1)S(1)} %copy-done.2, f32[2,32,128,128]{3,2,1,0:T(8,128)S(1)} %bitcast.9, bf16[64,128]{1,0:T(8,128)(2,1)S(1)} %copy-done.7, ...), custom_call_target="tpu_custom_call" | custom-call | tf_op jit(solution)/shard_map/facet_work/pallas_call | solution.py:443
  36.2 0.0 copy-start.1
  36.2 1.3 %copy-done.1 = bf16[16,512,128]{2,1,0:T(8,128)(2,1)} copy-done((bf16[16,512,128]{2,1,0:T(8,128)(2,1)}, bf16[16,512,128]{2,1,0:T(8,128)(2,1)S(1)}, u32[]{:S(2)}) %copy-start.1) | copy-done | bytes 2097176
  37.5 0.0 copy-start.3
  37.5 0.8 %copy-done.3 = bf16[16,2,64,128]{3,2,1,0:T(8,128)(2,1)} copy-done((bf16[16,2,64,128]{3,2,1,0:T(8,128)(2,1)}, bf16[16,2,64,128]{3,2,1,0:T(8,128)(2,1)S(1)}, u32[]{:S(2)}) %copy-start.3) | copy-done | bytes 524312
  38.3 27.5 %reduce_and_return.1 = (f32[512,128]{1,0:T(8,128)}, bf16[16,2,64,128]{3,2,1,0:T(8,128)(2,1)}) custom-call(bf16[16,512,128]{2,1,0:T(8,128)(2,1)} %copy-done.1, bf16[16,2,64,128]{3,2,1,0:T(8,128)(2,1)} %copy-done.3), custom_call_target="tpu_custom_call" | custom-call | tf_op jit(solution)/shard_map/reduce_and_return/pallas_call | solution.py:462
  65.9 0.0 copy-start.9
  65.9 6.2 %residual.1 = f32[16,2,512]{2,1,0:T(2,128)} custom-call(s32[16]{0:T(128)} %cnt.3, s32[16]{0:T(128)} %bitcast.13, f32[16,2,512]{2,1,0:T(2,128)} %vis.3, bf16[16,64,512]{2,1,0:T(8,128)(2,1)} %get-tuple-element.15.ku, bf16[16,64,512]{2,1,0:T(8,128)(2,1)} %get-tuple-element.16.kv, bf16[16,2,64,128]{3,2,1,0:T(8,128)(2,1)} %get-tuple-element.17.returned), custom_call_target="tpu_custom_call" | custom-call | tf_op jit(solution)/shard_map/residual/pallas_call | solution.py:486
  72.1 0.0 copy-done.9
  72.1 0.1 copy.16
  72.1 0.8 %reshape.13 = f32[1,8,2,4096]{3,2,1,0:T(2,128)} reshape(f32[8,2,32,128]{3,2,1,0:T(8,128)S(1)} %copy.16) | data formatting | bytes 524288 | tf_op jit(solution)/shard_map/reshape | solution.py:495
Async XLA Ops:
  5.5 18.7 %copy-start.4 = (bf16[128,128]{1,0:T(8,128)(2,1)S(1)}, bf16[128,128]{1,0:T(8,128)(2,1)}, u32[]{:S(2)}) copy-start(bf16[128,128]{1,0:T(8,128)(2,1)} %constant.11.clone.right_i) | copy-start | bytes 98308
  5.5 18.7 %copy-start.5 = (bf16[128,128]{1,0:T(8,128)(2,1)S(1)}, bf16[128,128]{1,0:T(8,128)(2,1)}, u32[]{:S(2)}) copy-start(bf16[128,128]{1,0:T(8,128)(2,1)} %constant.9.clone.right_f) | copy-start | bytes 98308
  5.6 18.7 %copy-start.6 = (bf16[64,128]{1,0:T(8,128)(2,1)S(1)}, bf16[64,128]{1,0:T(8,128)(2,1)}, u32[]{:S(2)}) copy-start(bf16[64,128]{1,0:T(8,128)(2,1)} %constant.10.clone.left_i) | copy-start | bytes 49156
  5.6 18.7 %copy-start.7 = (bf16[64,128]{1,0:T(8,128)(2,1)S(1)}, bf16[64,128]{1,0:T(8,128)(2,1)}, u32[]{:S(2)}) copy-start(bf16[64,128]{1,0:T(8,128)(2,1)} %constant.8.clone.left_f) | copy-start | bytes 49156
  24.3 2.2 %copy-start = (f32[128,2,32,128]{3,0,2,1:T(8,128)S(1)}, f32[128,2,32,128]{3,0,2,1:T(8,128)}, u32[]{:S(2)}) copy-start(f32[128,2,32,128]{3,0,2,1:T(8,128)} %copy.15) | copy-start | bytes 12582916
  26.4 1.0 %copy-start.2 = (bf16[16,2,64,128]{3,2,1,0:T(8,128)(2,1)S(1)}, bf16[16,2,64,128]{3,2,1,0:T(8,128)(2,1)}, u32[]{:S(2)}) copy-start(bf16[16,2,64,128]{3,2,1,0:T(8,128)(2,1)} %get-tuple-element.11.grid_in) | copy-start | bytes 1572868
  27.5 0.7 copy-start.8
  36.2 1.3 %copy-start.1 = (bf16[16,512,128]{2,1,0:T(8,128)(2,1)}, bf16[16,512,128]{2,1,0:T(8,128)(2,1)S(1)}, u32[]{:S(2)}) copy-start(bf16[16,512,128]{2,1,0:T(8,128)(2,1)S(1)} %get-tuple-element.12.canvas) | copy-start | bytes 6291460
  37.5 0.8 %copy-start.3 = (bf16[16,2,64,128]{3,2,1,0:T(8,128)(2,1)}, bf16[16,2,64,128]{3,2,1,0:T(8,128)(2,1)S(1)}, u32[]{:S(2)}) copy-start(bf16[16,2,64,128]{3,2,1,0:T(8,128)(2,1)S(1)} %get-tuple-element.13.back) | copy-start | bytes 1572868
  65.9 6.2 %copy-start.9 = (f32[512,128]{1,0:T(8,128)S(1)}, f32[512,128]{1,0:T(8,128)}, u32[]{:S(2)}) copy-start(f32[512,128]{1,0:T(8,128)} %get-tuple-element.14) | copy-start | bytes 786436

commit v2 on v1

--- a/solution.py
+++ b/solution.py
@@ -57,16 +57,18 @@
 
 def grid_kernel(
     facets, side, subgrids,
-    cnt, fid, row, col, vis, uv,
-    ku_out, kv_out, grid_in, meta_in,
-    grids, grid_send, meta_send, first, last,
-    send_sem, recv_sem, meta_send_sem, meta_recv_sem, own_sem,
+    cnt, fid, row, col, vis, uv, model,
+    ku_out, kv_out, grid_in, meta_in, planes,
+    grids, grid_send, meta_send, first, last, raw,
+    send_sem, recv_sem, meta_send_sem, meta_recv_sem, own_sem, raw_sem,
 ):
     me = lax.axis_index("facet")
     targets, sources = facet_peers(me, side)
     barrier = pltpu.get_barrier_semaphore()
     for peer in targets:
         pl.semaphore_signal(barrier, inc=1, device_id={"facet": peer})
+    fetch = pltpu.make_async_copy(model.at[0], raw, raw_sem)
+    fetch.start()
 
     ids = [fid[s] for s in range(subgrids)]
 
@@ -137,6 +139,15 @@
     own_meta = pltpu.make_async_copy(meta_send.at[me], meta_in.at[me], own_sem.at[1])
     own.start()
     own_meta.start()
+    fetch.wait()
+
+    def split(tile, carry):
+        at = pl.ds(pl.multiple_of(tile * LANES, LANES), LANES)
+        for part in range(2):
+            planes[part, tile] = raw[:, part, at].astype(jnp.float32)
+        return carry
+
+    lax.fori_loop(0, TILES, split, 0)
     for copy in started:
         copy.wait()
     own.wait()
@@ -157,8 +168,8 @@
 
 def facet_kernel(
     facets, chans,
-    meta, grid_in, model, left_f, right_f, left_i, right_i,
-    canvas_out, back_out,
+    meta, grid_in, left_f, right_f,
+    canvas_out,
     canvas, halves, patches,
 ):
     rows = F_ROWS // chans
@@ -228,49 +239,15 @@
 
     lax.fori_loop(0, TILES // 2, emit, 0)
 
-    def pick(facet, carry):
-        picked = []
-        for slot in range(SLOTS):
-            top = meta[facet, 0, 3 * slot + 1]
-            col = meta[facet, 0, 3 * slot + 2]
-            tile, shift = col // LANES, lax.rem(col, LANES)
-            after = jnp.minimum(tile + 1, TILES - 1)
-            at = pl.ds(top, SUB)
-            parts = [
-                jnp.where(lane >= shift, model[part, tile, at, :], model[part, after, at, :])
-                for part in range(2)
-            ]
-            re = pltpu.roll(parts[0], lax.rem(LANES - shift, LANES), 1)
-            im = pltpu.roll(parts[1], lax.rem(LANES + SUB - shift, LANES), 1)
-            picked.append(jnp.where(lane < SUB, re, im).astype(jnp.bfloat16))
-        out = left_pair(left_i[...], picked[0], picked[1])
-        halves[pl.ds(pl.multiple_of(facet * 2 * SUB, 2 * SUB), SUB), :] = out[:, :LANES]
-        halves[pl.ds(pl.multiple_of(facet * 2 * SUB + SUB, SUB), SUB), :] = out[:, LANES:]
-        return carry
-
-    lax.fori_loop(0, facets, pick, 0, unroll=2)
-
-    def inverse_right(block, carry):
-        at = pl.ds(pl.multiple_of(block * 256, 256), 256)
-        out = jnp.dot(halves[at, :], right_i[...], preferred_element_type=jnp.float32)
-        out = out.astype(jnp.bfloat16)
-        for i in range(2):
-            for slot in range(SLOTS):
-                begin = (2 * i + slot) * SUB
-                back_out[2 * block + i, slot] = out[begin : begin + SUB]
-        return carry
-
-    lax.fori_loop(0, facets * SLOTS * SUB // 256, inverse_right, 0, unroll=2)
-
 
 PIECES = 4
 
 
 def exchange_kernel(
-    facets, side, chans,
-    canvas, back,
-    total, returned,
-    pair_buf, send_buf, recv_buf,
+    facets, side, chans, subgrids,
+    meta, cnt, fid, canvas, planes, vis, ku, kv, left_i, right_i,
+    total, residual,
+    pair_buf, send_buf, recv_buf, halves, back, returned, rank,
     pair_send, pair_recv, ring_send, ring_recv, back_send, back_recv, own_sem,
 ):
     chips = chans // 2
@@ -285,6 +262,40 @@
         pl.semaphore_signal(barrier, inc=1, device_id={"chan": peer})
     for peer in targets:
         pl.semaphore_signal(barrier, inc=1, device_id={"facet": peer})
+
+    lane = lax.broadcasted_iota(jnp.int32, (SUB, LANES), 1)
+
+    def pick(facet, carry):
+        picked = []
+        for slot in range(SLOTS):
+            top = meta[facet, 0, 3 * slot + 1]
+            col = meta[facet, 0, 3 * slot + 2]
+            tile, shift = col // LANES, lax.rem(col, LANES)
+            after = jnp.minimum(tile + 1, TILES - 1)
+            at = pl.ds(top, SUB)
+            parts = [
+                jnp.where(lane >= shift, planes[part, tile, at, :], planes[part, after, at, :])
+                for part in range(2)
+            ]
+            re = pltpu.roll(parts[0], lax.rem(LANES - shift, LANES), 1)
+            im = pltpu.roll(parts[1], lax.rem(LANES + SUB - shift, LANES), 1)
+            picked.append(jnp.where(lane < SUB, re, im).astype(jnp.bfloat16))
+        out = left_pair(left_i[...], picked[0], picked[1])
+        halves[pl.ds(pl.multiple_of(facet * 2 * SUB, 2 * SUB), SUB), :] = out[:, :LANES]
+        halves[pl.ds(pl.multiple_of(facet * 2 * SUB + SUB, SUB), SUB), :] = out[:, LANES:]
+        return carry
+
+    def inverse_right(block, carry):
+        at = pl.ds(pl.multiple_of(block * 256, 256), 256)
+        out = jnp.dot(halves[at, :], right_i[...], preferred_element_type=jnp.float32)
+        out = out.astype(jnp.bfloat16)
+        for i in range(2):
+            for slot in range(SLOTS):
+                begin = (2 * i + slot) * SUB
+                back[2 * block + i, slot] = out[begin : begin + SUB]
+        return carry
+
+    lax.fori_loop(0, facets // 2, pick, 0, unroll=2)
     pl.semaphore_wait(barrier, 3 + facets - 1)
 
     half = chips // 2
@@ -292,7 +303,6 @@
     for d in range(half - 1, 0, -1):
         offsets += [d, chips - d]
     offsets += [0]
-    waits = []
     pair_copy = {}
     for offset in offsets:
         there = lax.rem(z + offset, chips)
@@ -302,13 +312,17 @@
         )
         copy.start()
         pair_copy[offset] = copy
+
+    lax.fori_loop(facets // 2, facets, pick, 0, unroll=2)
+    lax.fori_loop(0, facets * SLOTS * SUB // 256, inverse_right, 0, unroll=2)
+    back_copy = []
     for i, peer in enumerate(targets):
         copy = pltpu.make_async_remote_copy(
             src_ref=back.at[peer], dst_ref=returned.at[me_f],
             send_sem=back_send.at[i], recv_sem=back_recv.at[i], device_id={"facet": peer},
         )
         copy.start()
-        waits.append(copy)
+        back_copy.append(copy)
     own = pltpu.make_async_copy(back.at[me_f], returned.at[me_f], own_sem)
     own.start()
 
@@ -329,7 +343,8 @@
         return half - (piece + way) % 2
 
     ring = {}
-    for step in range(half + 1):
+
+    def ring_step(step):
         for piece in range(PIECES):
             for way in range(2):
                 count = length(piece, way)
@@ -350,6 +365,34 @@
                 )
                 copy.start()
                 ring[way, piece, step] = copy
+
+    def degrid(s, carry):
+        image = returned[fid[s], rank[s]]
+        inner = lax.dot_general(
+            image, ku[s], (((0,), (0,)), ((), ())), preferred_element_type=jnp.float32
+        )
+        weight = kv[s].astype(jnp.float32)
+        live = live_row(cnt[s])
+        for part in range(2):
+            predicted = jnp.sum(inner[part * SUB : (part + 1) * SUB] * weight, 0, keepdims=True)
+            residual[s, pl.ds(part, 1), :] = (vis[s, pl.ds(part, 1), :] - predicted) * live
+        return carry
+
+    ring_step(0)
+    ids = [fid[s] for s in range(subgrids)]
+    for s in range(subgrids):
+        before = jnp.int32(0)
+        for other in range(s):
+            before = jnp.where(ids[other] == ids[s], 1, before)
+        rank[s] = before
+    for step in range(1, half - 1):
+        ring_step(step)
+    for copy in back_copy:
+        copy.wait()
+    own.wait()
+    lax.fori_loop(0, subgrids // 2, degrid, 0, unroll=2)
+    ring_step(half - 1)
+    lax.fori_loop(subgrids // 2, subgrids, degrid, 0, unroll=2)
     for piece in range(PIECES):
         value = mine(0, piece)
         for way in range(2):
@@ -361,38 +404,11 @@
         copy.wait_send()
     for copy in ring.values():
         copy.wait_send()
-    for copy in waits:
-        copy.wait()
-    own.wait()
-
-
-def residual_kernel(subgrids, facets, cnt, fid, vis, ku, kv, returned, out, seen):
-    def clear(facet, carry):
-        seen[facet] = 0
-        return carry
-
-    lax.fori_loop(0, facets, clear, 0)
-
-    def one(s, carry):
-        facet = fid[s]
-        slot = seen[facet]
-        seen[facet] = slot + 1
-        image = returned[facet, slot]
-        inner = lax.dot_general(
-            image, ku[s], (((0,), (0,)), ((), ())), preferred_element_type=jnp.float32
-        )
-        weight = kv[s].astype(jnp.float32)
-        live = live_row(cnt[s])
-        for part in range(2):
-            predicted = jnp.sum(inner[part * SUB : (part + 1) * SUB] * weight, 0, keepdims=True)
-            out[s, pl.ds(part, 1), :] = (vis[s, pl.ds(part, 1), :] - predicted) * live
-        return carry
-
-    lax.fori_loop(0, subgrids, one, 0)
 
 
 VMEM = pl.BlockSpec(memory_space=pltpu.VMEM)
 SMEM = pl.BlockSpec(memory_space=pltpu.SMEM)
+HBM = pl.BlockSpec(memory_space=pltpu.HBM)
 
 
 def per_device(
@@ -406,71 +422,70 @@
     shape = jax.ShapeDtypeStruct
     left_f, right_f, left_i, right_i = (jnp.asarray(table) for table in dft_tables())
     ids = subgrid_facet[:, 0]
-    big = 60 << 20
-
-    ku, kv, grid_in, meta = pl.pallas_call(
+
+    ku, kv, grid_in, meta, planes = pl.pallas_call(
         functools.partial(grid_kernel, facets, side, subgrids),
         out_shape=(
             shape((subgrids, SUB, NV), jnp.bfloat16),
             shape((subgrids, SUB, NV), jnp.bfloat16),
             shape((facets, SLOTS, SUB, LANES), jnp.bfloat16),
             shape((facets, 1, LANES), jnp.int32),
+            shape((2, TILES, F_ROWS, LANES), jnp.float32),
         ),
-        in_specs=[SMEM] * 4 + [VMEM] * 2,
-        out_specs=(VMEM,) * 4,
+        in_specs=[SMEM] * 4 + [VMEM] * 2 + [HBM],
+        out_specs=(VMEM,) * 5,
         scratch_shapes=[
             pltpu.VMEM((subgrids, SUB, LANES), jnp.bfloat16),
             pltpu.VMEM((facets, SLOTS, SUB, LANES), jnp.bfloat16),
             pltpu.VMEM((facets, 1, LANES), jnp.int32),
             pltpu.SMEM((facets,), jnp.int32),
             pltpu.SMEM((facets,), jnp.int32),
+            pltpu.VMEM(model_facet.shape[1:], jnp.bfloat16),
             pltpu.SemaphoreType.DMA((facets - 1,)),
             pltpu.SemaphoreType.DMA((facets - 1,)),
             pltpu.SemaphoreType.DMA((facets - 1,)),
             pltpu.SemaphoreType.DMA((facets - 1,)),
             pltpu.SemaphoreType.DMA((2,)),
+            pltpu.SemaphoreType.DMA,
         ],
-        compiler_params=pltpu.CompilerParams(collective_id=0, has_side_effects=True),
+        compiler_params=pltpu.CompilerParams(
+            collective_id=0, has_side_effects=True, vmem_limit_bytes=16 << 20
+        ),
         name="grid_and_send",
-    )(vis_count, ids, row_offset, col_offset, visibility, uv_coords)
-
-    model = (
-        model_facet[0]
-        .reshape(F_ROWS, 2, TILES, LANES)
-        .transpose(1, 2, 0, 3)
-        .astype(jnp.float32)
-    )
-    canvas, back = pl.pallas_call(
+    )(vis_count, ids, row_offset, col_offset, visibility, uv_coords, model_facet)
+
+    canvas = pl.pallas_call(
         functools.partial(facet_kernel, facets, chans),
-        out_shape=(
-            shape((chans, 2 * TILES * rows, LANES), jnp.bfloat16),
-            shape((facets, SLOTS, SUB, LANES), jnp.bfloat16),
-        ),
-        in_specs=[SMEM] + [VMEM] * 6,
-        out_specs=(VMEM,) * 2,
+        out_shape=shape((chans, 2 * TILES * rows, LANES), jnp.bfloat16),
+        in_specs=[SMEM] + [VMEM] * 3,
+        out_specs=VMEM,
         scratch_shapes=[
             pltpu.VMEM((2, TILES + 1, F_ROWS, LANES), jnp.float32),
             pltpu.VMEM((facets * SLOTS * SUB, LANES), jnp.bfloat16),
             pltpu.VMEM((facets * SLOTS * SUB, LANES), jnp.float32),
         ],
-        compiler_params=pltpu.CompilerParams(vmem_limit_bytes=40 << 20),
+        compiler_params=pltpu.CompilerParams(vmem_limit_bytes=16 << 20),
         name="facet_work",
-    )(meta, grid_in, model, left_f, right_f, left_i, right_i)
+    )(meta, grid_in, left_f, right_f)
 
     depth = 2 * TILES * rows // PIECES
     links = 2 * PIECES * (chips // 2)
-    total, returned = pl.pallas_call(
-        functools.partial(exchange_kernel, facets, side, chans),
+    total, residual = pl.pallas_call(
+        functools.partial(exchange_kernel, facets, side, chans, subgrids),
         out_shape=(
             shape((2 * TILES * rows, LANES), jnp.float32),
-            shape((facets, SLOTS, SUB, LANES), jnp.bfloat16),
+            shape(visibility.shape, jnp.float32),
         ),
-        in_specs=[VMEM] * 2,
+        in_specs=[SMEM] * 3 + [VMEM] * 7,
         out_specs=(VMEM,) * 2,
         scratch_shapes=[
             pltpu.VMEM((chips, 2 * TILES * rows, LANES), jnp.bfloat16),
             pltpu.VMEM((links, depth, LANES), jnp.bfloat16),
             pltpu.VMEM((links, depth, LANES), jnp.bfloat16),
+            pltpu.VMEM((facets * SLOTS * SUB, LANES), jnp.bfloat16),
+            pltpu.VMEM((facets, SLOTS, SUB, LANES), jnp.bfloat16),
+            pltpu.VMEM((facets, SLOTS, SUB, LANES), jnp.bfloat16),
+            pltpu.SMEM((subgrids,), jnp.int32),
             pltpu.SemaphoreType.DMA((chips,)),
             pltpu.SemaphoreType.DMA((chips,)),
             pltpu.SemaphoreType.DMA((links,)),
@@ -479,18 +494,11 @@
             pltpu.SemaphoreType.DMA((facets - 1,)),
             pltpu.SemaphoreType.DMA,
         ],
-        compiler_params=pltpu.CompilerParams(collective_id=1, has_side_effects=True),
+        compiler_params=pltpu.CompilerParams(
+            collective_id=1, has_side_effects=True, vmem_limit_bytes=20 << 20
+        ),
         name="reduce_and_return",
-    )(canvas, back)
-
-    residual = pl.pallas_call(
-        functools.partial(residual_kernel, subgrids, facets),
-        out_shape=shape(visibility.shape, jnp.float32),
-        in_specs=[SMEM] * 2 + [VMEM] * 4,
-        out_specs=VMEM,
-        scratch_shapes=[pltpu.SMEM((facets,), jnp.int32)],
-        name="residual",
-    )(vis_count, ids, visibility, ku, kv, returned)
+    )(meta, vis_count, ids, canvas, planes, visibility, ku, kv, left_i, right_i)
 
     image = total.reshape(2, TILES, rows, LANES).transpose(2, 0, 1, 3).reshape(1, rows, 2, FACET)
     return image, residual

time: 74.4 us -> 54.9 us (0.74); the launches traced: 73 us -> 54.6 us
  Pallas kernels: 57.2 us -> 46.5 us
  local copies, waits for them, and re-layouts: 15.1 us -> 7.44 us
    pallas_call x2 -> x1, Pallas kernels: 33.7 us -> 28 us  [per_device(): pl.pallas_call(functools.partial(exchange_kernel, facets, side, chans, su...]
    unnamed x21 -> x29, local copies, waits for them, and re-layouts: 11 us -> 6.54 us
    pallas_call x1, Pallas kernels: 8 us -> 4.49 us  [per_device(): pl.pallas_call(functools.partial(facet_kernel, facets, chans), out_shape=...]
    convert_element_type x1 -> x0, local copies, waits for them, and re-layouts: 3.19 us -> none  [per_device(): model = model_facet[0].reshape(F_ROWS, 2, TILES, LANES).transpose(1, 2, 0...]
    pallas_call x1, Pallas kernels: 15.4 us -> 13.9 us  [per_device(): pl.pallas_call(functools.partial(grid_kernel, facets, side, subgrids), ou...]
where the time goes in v2:
time: 54.9 us; the launch traced here: 54.6 us
  Pallas kernels  46.5 us (85%)
  local copies, waits for them, and re-layouts  7.44 us (14%)
  between operations  0.76 us (1%)
    pallas_call x1, Pallas kernels, per_device(): pl.pallas_call(functools.partial(exchange_kernel, facets, side, chans, su...  28 us
    pallas_call x1, Pallas kernels, per_device(): pl.pallas_call(functools.partial(grid_kernel, facets, side, subgrids), ou...  13.9 us
    unnamed x29, local copies, waits for them, and re-layouts  6.54 us
    pallas_call x1, Pallas kernels, per_device(): pl.pallas_call(functools.partial(facet_kernel, facets, chans), out_shape=...  4.49 us

profile of v2, /device:TPU:2, one launch (start us, length us, event | category | flops | bytes accessed | tf_op | source)
XLA Modules:
  0.0 54.6 jit_solution(14445646372625535713)
XLA Ops:
  0.6 0.0 copy-start
  0.6 1.6 %copy-done = bf16[1,128,2,4096]{3,2,1,0:T(2,128)(2,1)S(1)} copy-done((bf16[1,128,2,4096]{3,2,1,0:T(2,128)(2,1)S(1)}, bf16[1,128,2,4096]{3,2,1,0:T(2,128)(2,1)}, u32[]{:S(2)}) %copy-start) | copy-done | bytes 2097176
  2.2 0.0 copy-start.1
  2.2 0.8 %copy-done.1 = f32[16,2,512]{2,1,0:T(2,128)S(1)} copy-done((f32[16,2,512]{2,1,0:T(2,128)S(1)}, f32[16,2,512]{2,1,0:T(2,128)}, u32[]{:S(2)}) %copy-start.1) | copy-done | bytes 65560
  3.1 0.0 copy-start.3
  3.1 0.8 %copy-done.3 = f32[16,2,512]{2,1,0:T(2,128)S(1)} copy-done((f32[16,2,512]{2,1,0:T(2,128)S(1)}, f32[16,2,512]{2,1,0:T(2,128)}, u32[]{:S(2)}) %copy-start.3) | copy-done | bytes 65560
  3.9 0.0 copy-start.8
  3.9 0.7 %copy-done.8 = s32[16]{0:T(128)S(1)} copy-done((s32[16]{0:T(128)S(1)}, s32[16]{0:T(128)}, u32[]{:S(2)}) %copy-start.8) | copy-done | bytes 88
  4.6 0.0 copy-start.10
  4.6 0.7 %copy-done.10 = s32[16,1]{0,1:T(1,128)S(1)} copy-done((s32[16,1]{0,1:T(1,128)S(1)}, s32[16,1]{0,1:T(1,128)}, u32[]{:S(2)}) %copy-start.10) | copy-done | bytes 88
  5.2 0.0 copy-start.12
  5.2 0.7 %copy-done.12 = s32[16]{0:T(128)S(1)} copy-done((s32[16]{0:T(128)S(1)}, s32[16]{0:T(128)}, u32[]{:S(2)}) %copy-start.12) | copy-done | bytes 88
  5.9 0.0 copy-start.13
  5.9 0.7 %copy-done.13 = s32[16]{0:T(128)S(1)} copy-done((s32[16]{0:T(128)S(1)}, s32[16]{0:T(128)}, u32[]{:S(2)}) %copy-start.13) | copy-done | bytes 88
  6.5 0.0 copy-start.6
  6.5 0.0 copy-start.2
  6.5 0.0 copy-start.7
  6.6 0.0 copy-start.9
  6.6 0.0 copy-start.11
  6.6 13.9 %grid_and_send.1 = (bf16[16,64,512]{2,1,0:T(8,128)(2,1)S(1)}, bf16[16,64,512]{2,1,0:T(8,128)(2,1)S(1)}, bf16[16,2,64,128]{3,2,1,0:T(8,128)(2,1)S(1)}, s32[16,1,128]{2,1,0:T(1,128)S(1)}, f32[2,32,128,128]{3,2,1,0:T(8,128)S(1)}) custom-call(s32[16]{0:T(128)S(1)} %copy-done.8, s32[16]{0:T(128)S(1)} %bitcast.7, s32[16]{0:T(128)S(1)} %copy-done.12, ...), custom_call_target="tpu_custom_call" | custom-call | tf_op jit(solution)/shard_map/grid_and_send/pallas_call | solution.py:426
  20.5 0.0 copy-done.4
  20.5 0.0 copy-done.6
  20.5 4.5 %facet_work.1.canvas = bf16[16,512,128]{2,1,0:T(8,128)(2,1)S(1)} custom-call(s32[16,1,128]{2,1,0:T(1,128)S(1)} %get-tuple-element.9.meta, bf16[16,2,64,128]{3,2,1,0:T(8,128)(2,1)S(1)} %get-tuple-element.10.grid_in, bf16[64,128]{1,0:T(8,128)(2,1)S(1)} %copy-done.6, bf16[128,128]{1,0:T(8,128)(2,1)S(1)} %copy-done.4), custom_call_target="tpu_custom_call" | custom-call | tf_op jit(solution)/shard_map/facet_work/pallas_call | solution.py:457
  25.0 0.0 copy-done.2
  25.1 0.0 copy-done.5
  25.1 0.0 copy-done.7
  25.1 0.0 copy-done.9
  25.1 0.0 copy-done.11
  25.1 28.0 %reduce_and_return.1 = (f32[512,128]{1,0:T(8,128)S(1)}, f32[16,2,512]{2,1,0:T(2,128)S(1)}) custom-call(s32[16,1,128]{2,1,0:T(1,128)S(1)} %get-tuple-element.9.meta, s32[16]{0:T(128)S(1)} %copy-done.9, s32[16]{0:T(128)S(1)} %bitcast.8, bf16[16,512,128]{2,1,0:T(8,128)(2,1)S(1)} %facet_work.1.canvas, f32[2,32,128,128]{3,2,1,0:T(8,128)S(1)} %get-tuple-element.11.planes, ...), custom_call_target="tpu_custom_call" | custom-call | tf_op jit(solution)/shard_map/reduce_and_return/pallas_call | solution.py:473
  53.1 0.1 copy.13
  53.2 0.8 %reshape.11 = f32[1,8,2,4096]{3,2,1,0:T(2,128)} reshape(f32[8,2,32,128]{3,2,1,0:T(8,128)S(1)} %copy.13) | data formatting | bytes 524288 | tf_op jit(solution)/shard_map/reshape | solution.py:503
  54.0 0.6 %copy.15 = f32[16,2,512]{2,1,0:T(2,128)} copy(f32[16,2,512]{2,1,0:T(2,128)S(1)} %get-tuple-element.19) | data formatting | bytes 131072
  (2 shorter events, 0.0 us)
Async XLA Ops:
  0.6 1.6 %copy-start = (bf16[1,128,2,4096]{3,2,1,0:T(2,128)(2,1)S(1)}, bf16[1,128,2,4096]{3,2,1,0:T(2,128)(2,1)}, u32[]{:S(2)}) copy-start(bf16[1,128,2,4096]{3,2,1,0:T(2,128)(2,1)} %model.1) | copy-start | bytes 6291460
  2.2 0.8 %copy-start.1 = (f32[16,2,512]{2,1,0:T(2,128)S(1)}, f32[16,2,512]{2,1,0:T(2,128)}, u32[]{:S(2)}) copy-start(f32[16,2,512]{2,1,0:T(2,128)} %vis.3) | copy-start | bytes 196612
  3.1 0.8 %copy-start.3 = (f32[16,2,512]{2,1,0:T(2,128)S(1)}, f32[16,2,512]{2,1,0:T(2,128)}, u32[]{:S(2)}) copy-start(f32[16,2,512]{2,1,0:T(2,128)} %uv.1) | copy-start | bytes 196612
  3.9 0.7 %copy-start.8 = (s32[16]{0:T(128)S(1)}, s32[16]{0:T(128)}, u32[]{:S(2)}) copy-start(s32[16]{0:T(128)} %cnt.3) | copy-start | bytes 196
  4.6 0.7 %copy-start.10 = (s32[16,1]{0,1:T(1,128)S(1)}, s32[16,1]{0,1:T(1,128)}, u32[]{:S(2)}) copy-start(s32[16,1]{0,1:T(1,128)} %param.14) | copy-start | bytes 196
  5.2 0.7 %copy-start.12 = (s32[16]{0:T(128)S(1)}, s32[16]{0:T(128)}, u32[]{:S(2)}) copy-start(s32[16]{0:T(128)} %row.1) | copy-start | bytes 196
  5.9 0.7 %copy-start.13 = (s32[16]{0:T(128)S(1)}, s32[16]{0:T(128)}, u32[]{:S(2)}) copy-start(s32[16]{0:T(128)} %col.1) | copy-start | bytes 196
  6.5 14.0 %copy-start.4 = (bf16[128,128]{1,0:T(8,128)(2,1)S(1)}, bf16[128,128]{1,0:T(8,128)(2,1)}, u32[]{:S(2)}) copy-start(bf16[128,128]{1,0:T(8,128)(2,1)} %constant.9.clone.right_f) | copy-start | bytes 98308
  6.5 14.0 %copy-start.6 = (bf16[64,128]{1,0:T(8,128)(2,1)S(1)}, bf16[64,128]{1,0:T(8,128)(2,1)}, u32[]{:S(2)}) copy-start(bf16[64,128]{1,0:T(8,128)(2,1)} %constant.8.clone.left_f) | copy-start | bytes 49156
  6.5 18.5 %copy-start.2 = (f32[16,2,512]{2,1,0:T(2,128)S(1)}, f32[16,2,512]{2,1,0:T(2,128)}, u32[]{:S(2)}) copy-start(f32[16,2,512]{2,1,0:T(2,128)} %vis.3) | copy-start | bytes 196612
  6.5 18.5 %copy-start.5 = (bf16[128,128]{1,0:T(8,128)(2,1)S(1)}, bf16[128,128]{1,0:T(8,128)(2,1)}, u32[]{:S(2)}) copy-start(bf16[128,128]{1,0:T(8,128)(2,1)} %constant.11.clone.right_i) | copy-start | bytes 98308
  6.5 18.5 %copy-start.7 = (bf16[64,128]{1,0:T(8,128)(2,1)S(1)}, bf16[64,128]{1,0:T(8,128)(2,1)}, u32[]{:S(2)}) copy-start(bf16[64,128]{1,0:T(8,128)(2,1)} %constant.10.clone.left_i) | copy-start | bytes 49156
  6.6 18.5 %copy-start.9 = (s32[16]{0:T(128)S(1)}, s32[16]{0:T(128)}, u32[]{:S(2)}) copy-start(s32[16]{0:T(128)} %cnt.3) | copy-start | bytes 196
  6.6 18.5 %copy-start.11 = (s32[16,1]{0,1:T(1,128)S(1)}, s32[16,1]{0,1:T(1,128)}, u32[]{:S(2)}) copy-start(s32[16,1]{0,1:T(1,128)} %param.14) | copy-start | bytes 196

commit v3 on v2

v3 whole, which is shorter than its diff:
```python
import functools
import math

import jax
import jax.numpy as jnp
import numpy as np
from jax import lax
from jax.experimental import pallas as pl
from jax.experimental.pallas import tpu as pltpu
from jax.sharding import PartitionSpec as P

SUB = 64
FACET = 4096
F_ROWS = 128
NV = 512
LANES = 128
TILES = FACET // LANES
SLOTS = 2


def dft_tables():
    line = np.arange(SUB)
    angle = 2.0 * math.pi * (line[:, None] * line[None, :] % SUB) / SUB
    cos_table = (np.cos(angle) / math.sqrt(SUB)).astype(jnp.bfloat16)
    sin_table = (-np.sin(angle) / math.sqrt(SUB)).astype(jnp.bfloat16)
    left_forward = np.concatenate([cos_table, sin_table], 1)
    left_inverse = np.concatenate([cos_table, -sin_table], 1)
    right_forward = np.concatenate(
        [np.concatenate([cos_table, sin_table], 1), np.concatenate([-sin_table, cos_table], 1)], 0
    )
    right_inverse = np.concatenate(
        [np.concatenate([cos_table, -sin_table], 1), np.concatenate([sin_table, cos_table], 1)], 0
    )
    return left_forward, right_forward, left_inverse, right_inverse


def kernel_of(coords):
    pixels = lax.broadcasted_iota(jnp.int32, (SUB, NV), 0).astype(jnp.float32)
    delta = pixels - coords
    return jnp.exp(-(delta * delta))


def live_row(count):
    lane = lax.broadcasted_iota(jnp.int32, (1, NV), 1)
    return (lane < count).astype(jnp.float32)


def facet_steps(me, side):
    x, y = me // side, lax.rem(me, side)
    targets, sources = [], []
    for step in range(1, side * side):
        dx, dy = step // side, step % side
        targets.append(lax.rem(x + dx, side) * side + lax.rem(y + dy, side))
        sources.append(lax.rem(x + side - dx, side) * side + lax.rem(y + side - dy, side))
    return targets, sources


def swapped(values):
    half = values.shape[-1] // 2
    return jnp.concatenate([-values[:, half:], values[:, :half]], 1)


def left_pair(table, one, two):
    upper = jnp.concatenate([one, two], 1)
    lower = jnp.concatenate([swapped(one), swapped(two)], 1)
    out = jnp.dot(table, jnp.concatenate([upper, lower], 0), preferred_element_type=jnp.float32)
    return out.astype(jnp.bfloat16)


def gridded(lines):
    ku = kernel_of(lines[2:3]).astype(jnp.bfloat16)
    kv = kernel_of(lines[3:4])
    spread = jnp.concatenate(
        [(lines[0:1] * kv).astype(jnp.bfloat16), (lines[1:2] * kv).astype(jnp.bfloat16)], 0
    )
    return lax.dot_general(
        ku, spread, (((1,), (1,)), ((), ())), preferred_element_type=jnp.float32
    ).astype(jnp.bfloat16)


GROUP = 2


def grid_kernel(
    facets, side, subgrids,
    cnt_hbm, fid_hbm, row_hbm, col_hbm, vis_hbm, uv_hbm, model, left_hbm, right_hbm,
    patches, meta_in, model_rows,
    cnt, fid, row, col, vis, uv, left_f, right_f, raw, lines_send, lines_in, meta_send, first, last,
    in_sem, raw_sem, send_sem, recv_sem, meta_send_sem, meta_recv_sem, own_sem,
):
    me = lax.axis_index("facet")
    targets, _ = facet_steps(me, side)
    barrier = pltpu.get_barrier_semaphore()
    for peer in targets:
        pl.semaphore_signal(barrier, inc=1, device_id={"facet": peer})
    fetches = []
    for i, (src, dst) in enumerate((
        (fid_hbm, fid), (cnt_hbm, cnt), (row_hbm, row), (col_hbm, col), (vis_hbm, vis), (uv_hbm, uv),
        (left_hbm, left_f), (right_hbm, right_f),
    )):
        fetch = pltpu.make_async_copy(src, dst, in_sem.at[i])
        fetch.start()
        fetches.append(fetch)

    def model_copy(tile):
        at = pl.ds(pl.multiple_of(tile * LANES, LANES), LANES)
        return pltpu.make_async_copy(model.at[0, :, :, at], raw.at[tile], raw_sem.at[tile])

    def fetch_model(tile, carry):
        model_copy(tile).start()
        return carry

    lax.fori_loop(0, TILES, fetch_model, 0)
    for fetch in fetches:
        fetch.wait()

    ids = [fid[s] for s in range(subgrids)]

    def find(facet, carry):
        low = jnp.int32(subgrids)
        high = jnp.int32(-1)
        for s in range(subgrids):
            high = jnp.where(ids[s] == facet, s, high)
            back = subgrids - 1 - s
            low = jnp.where(ids[back] == facet, back, low)
        first[facet] = low
        last[facet] = high
        return carry

    lax.fori_loop(0, facets, find, 0)

    lane = lax.broadcasted_iota(jnp.int32, (1, LANES), 1)

    def pack(facet, carry):
        low, high = first[facet], last[facet]
        one = jnp.minimum(low, subgrids - 1)
        two = jnp.maximum(high, 0)
        lines_send[facet] = jnp.concatenate(
            [vis[one] * live_row(cnt[one]), uv[one], vis[two] * live_row(cnt[two]), uv[two]], 0
        )
        values = (
            (high >= 0).astype(jnp.int32), row[one], col[one],
            (high > low).astype(jnp.int32), row[two], col[two],
        )
        line = jnp.zeros((1, LANES), jnp.int32)
        for place, value in enumerate(values):
            line = jnp.where(lane == place, value, line)
        meta_send[facet] = line
        return carry

    lax.fori_loop(0, facets, pack, 0)

    pl.semaphore_wait(barrier, facets - 1)
    copies = [None]
    metas = []
    for step, peer in enumerate(targets, 1):
        pair = []
        for src, dst, ssem, rsem in (
            (meta_send, meta_in, meta_send_sem, meta_recv_sem),
            (lines_send, lines_in, send_sem, recv_sem),
        ):
            copy = pltpu.make_async_remote_copy(
                src_ref=src.at[peer], dst_ref=dst.at[step], send_sem=ssem.at[step],
                recv_sem=rsem.at[step], device_id={"facet": peer},
            )
            copy.start()
            pair.append(copy)
        metas.append(pair[0])
        copies.append(pair[1])
    own = pltpu.make_async_copy(lines_send.at[me], lines_in.at[0], own_sem.at[0])
    own_meta = pltpu.make_async_copy(meta_send.at[me], meta_in.at[0], own_sem.at[1])
    own.start()
    own_meta.start()

    rows_view = raw.reshape(TILES, 2 * F_ROWS, LANES)

    def widen(tile, carry):
        model_copy(tile).wait()
        model_rows[tile] = rows_view[tile].astype(jnp.float32)
        return carry

    lax.fori_loop(0, TILES, widen, 0)

    own.wait()
    own_meta.wait()
    for begin in range(0, facets, GROUP):
        halves = []
        for step in range(begin, begin + GROUP):
            if step > 0:
                copies[step].wait_recv()
        for step in range(begin, begin + GROUP):
            lines = lines_in[step]
            out = left_pair(left_f[...], gridded(lines[:4]), gridded(lines[4:]))
            halves += [out[:, :LANES], out[:, LANES:]]
        out = jnp.dot(
            jnp.concatenate(halves, 0), right_f[...], preferred_element_type=jnp.float32
        )
        patches[pl.ds(begin * SLOTS * SUB, GROUP * SLOTS * SUB), :] = out
    for copy in copies[1:]:
        copy.wait_send()
    for copy in metas:
        copy.wait()


def add_kernel(facets, meta, patches, canvas):
    lane = lax.broadcasted_iota(jnp.int32, (SUB, LANES), 1)
    zero = jnp.zeros((F_ROWS, LANES), jnp.float32)

    def clear(tile, carry):
        canvas[0, tile] = zero
        canvas[1, tile] = zero
        return carry

    lax.fori_loop(0, TILES, clear, 0)

    def add(step, carry):
        for slot in range(SLOTS):
            valid = meta[step, 0, 3 * slot]

            @pl.when(valid > 0)
            def _():
                top = meta[step, 0, 3 * slot + 1]
                col = meta[step, 0, 3 * slot + 2]
                tile, shift = col // LANES, lax.rem(col, LANES)
                patch = patches[pl.ds(pl.multiple_of((step * 2 + slot) * SUB, SUB), SUB), :]
                inside = (lane >= shift) & (lane < shift + SUB)
                at = pl.ds(top, SUB)
                turned = (
                    pltpu.roll(patch, shift, 1),
                    pltpu.roll(patch, lax.rem(shift + SUB, LANES), 1),
                )
                for part in range(2):
                    canvas[part, tile, at, :] += jnp.where(inside, turned[part], 0.0)

                @pl.when(shift > SUB)
                def _():
                    beyond = lane < shift - SUB
                    for part in range(2):
                        canvas[part, tile + 1, at, :] += jnp.where(beyond, turned[part], 0.0)

        return carry

    lax.fori_loop(0, facets, add, 0)


PIECES = 4


def exchange_kernel(
    facets, side, chans, subgrids,
    meta, cnt, fid, canvas, model_rows, vis, uv, left_i, right_i,
    total, residual,
    half_buf, pair_buf, send_buf, recv_buf, halves, back, returned, place,
    pair_send, pair_recv, ring_send, ring_recv, back_send, back_recv, own_sem,
):
    chips = chans // 2
    me_f, me_c = lax.axis_index("facet"), lax.axis_index("chan")
    z, core = me_c // 2, lax.rem(me_c, 2)
    partner = z * 2 + 1 - core
    right = lax.rem(z + 1, chips) * 2 + core
    left = lax.rem(z + chips - 1, chips) * 2 + core
    targets, sources = facet_steps(me_f, side)
    rows = F_ROWS // chans
    barrier = pltpu.get_barrier_semaphore()
    for peer in (partner, right, left):
        pl.semaphore_signal(barrier, inc=1, device_id={"chan": peer})
    for peer in targets:
        pl.semaphore_signal(barrier, inc=1, device_id={"facet": peer})

    lane = lax.broadcasted_iota(jnp.int32, (SUB, LANES), 1)

    def pick(facet, carry):
        picked = []
        for slot in range(SLOTS):
            top = meta[facet, 0, 3 * slot + 1]
            col = meta[facet, 0, 3 * slot + 2]
            tile, shift = col // LANES, lax.rem(col, LANES)
            after = jnp.minimum(tile + 1, TILES - 1)
            parts = [
                jnp.where(
                    lane >= shift,
                    model_rows[tile, pl.ds(2 * top + part, SUB, stride=2), :],
                    model_rows[after, pl.ds(2 * top + part, SUB, stride=2), :],
                )
                for part in range(2)
            ]
            re = pltpu.roll(parts[0], lax.rem(LANES - shift, LANES), 1)
            im = pltpu.roll(parts[1], lax.rem(LANES + SUB - shift, LANES), 1)
            picked.append(jnp.where(lane < SUB, re, im).astype(jnp.bfloat16))
        out = left_pair(left_i[...], picked[0], picked[1])
        halves[pl.ds(pl.multiple_of(facet * 2 * SUB, 2 * SUB), SUB), :] = out[:, :LANES]
        halves[pl.ds(pl.multiple_of(facet * 2 * SUB + SUB, SUB), SUB), :] = out[:, LANES:]
        return carry

    def inverse_right(block, carry):
        at = pl.ds(pl.multiple_of(block * 256, 256), 256)
        out = jnp.dot(halves[at, :], right_i[...], preferred_element_type=jnp.float32)
        out = out.astype(jnp.bfloat16)
        for i in range(2):
            for slot in range(SLOTS):
                begin = (2 * i + slot) * SUB
                back[2 * block + i, slot] = out[begin : begin + SUB]
        return carry

    half = chips // 2
    offsets = [half]
    for d in range(half - 1, 0, -1):
        offsets += [d, chips - d]
    offsets += [0]

    def chan_rows(offset, which):
        there = lax.rem(z + offset, chips)
        return pl.ds(pl.multiple_of((2 * there + which) * rows, rows), rows)

    def narrow(pair, carry):
        for offset in range(chips):
            for part in range(2):
                both = canvas[part, pl.ds(2 * pair, 2), chan_rows(offset, 1 - core), :]
                at = pl.ds(pl.multiple_of((part * TILES + 2 * pair) * rows, 2 * rows), 2 * rows)
                half_buf[offset, at, :] = both.reshape(2 * rows, LANES).astype(jnp.bfloat16)
        return carry

    lax.fori_loop(0, TILES // 2, narrow, 0)
    pl.semaphore_wait(barrier, 3 + facets - 1)

    pair_copy = {}
    for offset in offsets:
        copy = pltpu.make_async_remote_copy(
            src_ref=half_buf.at[offset], dst_ref=pair_buf.at[offset],
            send_sem=pair_send.at[offset], recv_sem=pair_recv.at[offset], device_id={"chan": partner},
        )
        copy.start()
        pair_copy[offset] = copy

    lax.fori_loop(0, facets // 2, pick, 0, unroll=2)

    depth = half_buf.shape[1] // PIECES
    arrived = set()

    def mine(offset, piece):
        if offset not in arrived:
            arrived.add(offset)
            pair_copy[offset].wait_recv()
        at = pl.ds(piece * depth, depth)
        tiles = TILES * 2 // PIECES
        part, begin = divmod(piece * tiles, TILES)
        own = canvas[part, pl.ds(begin, tiles), chan_rows(offset, core), :]
        return own.reshape(depth, LANES) + pair_buf[offset, at, :].astype(jnp.float32)

    def length(piece, way):
        return half - (piece + way) % 2

    ring = {}

    def ring_step(step):
        for piece in range(PIECES):
            for way in range(2):
                count = length(piece, way)
                if step >= count:
                    continue
                distance = count - step
                offset = distance if way == 0 else chips - distance
                value = mine(offset % chips, piece)
                slot = (way * PIECES + piece) * half + step
                if step > 0:
                    ring[way, piece, step - 1].wait_recv()
                    value = value + recv_buf[slot - 1].astype(jnp.float32)
                send_buf[slot] = value.astype(jnp.bfloat16)
                copy = pltpu.make_async_remote_copy(
                    src_ref=send_buf.at[slot], dst_ref=recv_buf.at[slot],
                    send_sem=ring_send.at[slot], recv_sem=ring_recv.at[slot],
                    device_id={"chan": right if way == 0 else left},
                )
                copy.start()
                ring[way, piece, step] = copy

    def degrid(s, carry):
        image = returned[place[s], place[subgrids + s]]
        ku = kernel_of(uv[s, pl.ds(0, 1), :]).astype(jnp.bfloat16)
        weight = kernel_of(uv[s, pl.ds(1, 1), :])
        inner = lax.dot_general(
            image, ku, (((0,), (0,)), ((), ())), preferred_element_type=jnp.float32
        )
        live = live_row(cnt[s])
        for part in range(2):
            predicted = jnp.sum(inner[part * SUB : (part + 1) * SUB] * weight, 0, keepdims=True)
            residual[s, pl.ds(part, 1), :] = (vis[s, pl.ds(part, 1), :] - predicted) * live
        return carry

    ring_step(0)
    lax.fori_loop(facets // 2, facets, pick, 0, unroll=2)
    lax.fori_loop(0, facets * SLOTS * SUB // 256, inverse_right, 0, unroll=2)
    back_copy = []
    for step in range(1, facets):
        copy = pltpu.make_async_remote_copy(
            src_ref=back.at[step], dst_ref=returned.at[step],
            send_sem=back_send.at[step], recv_sem=back_recv.at[step],
            device_id={"facet": sources[step - 1]},
        )
        copy.start()
        back_copy.append(copy)
    own = pltpu.make_async_copy(back.at[0], returned.at[0], own_sem)
    own.start()
    ring_step(1)
    ids = [fid[s] for s in range(subgrids)]
    x, y = me_f // side, lax.rem(me_f, side)
    for s in range(subgrids):
        before = jnp.int32(0)
        for other in range(s):
            before = jnp.where(ids[other] == ids[s], 1, before)
        there_x, there_y = ids[s] // side, lax.rem(ids[s], side)
        place[s] = lax.rem(there_x + side - x, side) * side + lax.rem(there_y + side - y, side)
        place[subgrids + s] = before
    ring_step(2)
    for copy in back_copy:
        copy.wait()
    own.wait()
    lax.fori_loop(0, subgrids // 2, degrid, 0, unroll=2)
    ring_step(3)
    lax.fori_loop(subgrids // 2, subgrids, degrid, 0, unroll=2)
    for piece in range(PIECES):
        value = mine(0, piece)
        for way in range(2):
            step = length(piece, way) - 1
            ring[way, piece, step].wait_recv()
            value = value + recv_buf[(way * PIECES + piece) * half + step].astype(jnp.float32)
        total[pl.ds(piece * depth, depth), :] = value
    for copy in pair_copy.values():
        copy.wait_send()
    for copy in ring.values():
        copy.wait_send()


VMEM = pl.BlockSpec(memory_space=pltpu.VMEM)
SMEM = pl.BlockSpec(memory_space=pltpu.SMEM)
HBM = pl.BlockSpec(memory_space=pltpu.HBM)


def per_device(
    visibility, uv_coords, vis_count, subgrid_facet, row_offset, col_offset, model_facet
):
    facets, chans = lax.axis_size("facet"), lax.axis_size("chan")
    side = math.isqrt(facets)
    chips = chans // 2
    subgrids = visibility.shape[0]
    rows = F_ROWS // chans
    shape = jax.ShapeDtypeStruct
    left_f, right_f, left_i, right_i = (jnp.asarray(table) for table in dft_tables())
    ids = subgrid_facet[:, 0]

    lines = (facets, SLOTS * 4, NV)
    patches, meta, model_rows = pl.pallas_call(
        functools.partial(grid_kernel, facets, side, subgrids),
        out_shape=(
            shape((facets * SLOTS * SUB, LANES), jnp.float32),
            shape((facets, 1, LANES), jnp.int32),
            shape((TILES, 2 * F_ROWS, LANES), jnp.float32),
        ),
        in_specs=[HBM] * 9,
        out_specs=(VMEM,) * 3,
        scratch_shapes=[
            pltpu.SMEM((subgrids,), jnp.int32),
            pltpu.SMEM((subgrids,), jnp.int32),
            pltpu.SMEM((subgrids,), jnp.int32),
            pltpu.SMEM((subgrids,), jnp.int32),
            pltpu.VMEM(visibility.shape, jnp.float32),
            pltpu.VMEM(uv_coords.shape, jnp.float32),
            pltpu.VMEM(left_f.shape, jnp.bfloat16),
            pltpu.VMEM(right_f.shape, jnp.bfloat16),
            pltpu.VMEM((TILES, F_ROWS, 2, LANES), jnp.bfloat16),
            pltpu.VMEM(lines, jnp.float32),
            pltpu.VMEM(lines, jnp.float32),
            pltpu.VMEM((facets, 1, LANES), jnp.int32),
            pltpu.SMEM((facets,), jnp.int32),
            pltpu.SMEM((facets,), jnp.int32),
            pltpu.SemaphoreType.DMA((8,)),
            pltpu.SemaphoreType.DMA((TILES,)),
            pltpu.SemaphoreType.DMA((facets,)),
            pltpu.SemaphoreType.DMA((facets,)),
            pltpu.SemaphoreType.DMA((facets,)),
            pltpu.SemaphoreType.DMA((facets,)),
            pltpu.SemaphoreType.DMA((2,)),
        ],
        compiler_params=pltpu.CompilerParams(
            collective_id=0, has_side_effects=True, vmem_limit_bytes=16 << 20
        ),
        name="grid_and_send",
    )(
        *(
            pltpu.with_memory_space_constraint(array, pltpu.HBM)
            for array in (
                vis_count, ids, row_offset, col_offset, visibility, uv_coords, model_facet,
                left_f, right_f,
            )
        )
    )

    canvas = pl.pallas_call(
        functools.partial(add_kernel, facets),
        out_shape=shape((2, TILES, F_ROWS, LANES), jnp.float32),
        in_specs=[SMEM, VMEM],
        out_specs=VMEM,
        compiler_params=pltpu.CompilerParams(vmem_limit_bytes=16 << 20),
        name="add_windows",
    )(meta, patches)

    depth = 2 * TILES * rows // PIECES
    links = 2 * PIECES * (chips // 2)
    total, residual = pl.pallas_call(
        functools.partial(exchange_kernel, facets, side, chans, subgrids),
        out_shape=(
            shape((2 * TILES * rows, LANES), jnp.float32),
            shape(visibility.shape, jnp.float32),
        ),
        in_specs=[SMEM] * 3 + [VMEM] * 6,
        out_specs=(VMEM,) * 2,
        scratch_shapes=[
            pltpu.VMEM((chips, 2 * TILES * rows, LANES), jnp.bfloat16),
            pltpu.VMEM((chips, 2 * TILES * rows, LANES), jnp.bfloat16),
            pltpu.VMEM((links, depth, LANES), jnp.bfloat16),
            pltpu.VMEM((links, depth, LANES), jnp.bfloat16),
            pltpu.VMEM((facets * SLOTS * SUB, LANES), jnp.bfloat16),
            pltpu.VMEM((facets, SLOTS, SUB, LANES), jnp.bfloat16),
            pltpu.VMEM((facets, SLOTS, SUB, LANES), jnp.bfloat16),
            pltpu.SMEM((2 * subgrids,), jnp.int32),
            pltpu.SemaphoreType.DMA((chips,)),
            pltpu.SemaphoreType.DMA((chips,)),
            pltpu.SemaphoreType.DMA((links,)),
            pltpu.SemaphoreType.DMA((links,)),
            pltpu.SemaphoreType.DMA((facets,)),
            pltpu.SemaphoreType.DMA((facets,)),
            pltpu.SemaphoreType.DMA,
        ],
        compiler_params=pltpu.CompilerParams(
            collective_id=1, has_side_effects=True, vmem_limit_bytes=20 << 20
        ),
        name="reduce_and_return",
    )(meta, vis_count, ids, canvas, model_rows, visibility, uv_coords, left_i, right_i)

    image = total.reshape(2, TILES, rows, LANES).transpose(2, 0, 1, 3).reshape(1, rows, 2, FACET)
    return image, residual


def solution(mesh):
    in_specs = (
        P(("facet", "chan"), None, None),
        P(("facet", "chan"), None, None),
        P(("facet", "chan")),
        P(("facet", "chan"), None),
        P(("facet", "chan")),
        P(("facet", "chan")),
        P("facet", None, None, None),
    )
    out_specs = (P("facet", "chan", None, None), P(("facet", "chan"), None, None))
    return jax.shard_map(
        per_device, mesh=mesh, in_specs=in_specs, out_specs=out_specs, check_vma=False
    )
```

time: 54.9 us -> 50.9 us (0.927)
  local copies, waits for them, and re-layouts: 7.44 us -> 1.55 us
  Pallas kernels: 46.5 us -> 48.5 us
    unnamed x29 -> x13, local copies, waits for them, and re-layouts: 6.54 us -> 0.66 us
    pallas_call x1, Pallas kernels: 13.9 us -> 16.9 us  [per_device(): pl.pallas_call(functools.partial(grid_kernel, facets, side, subgrids), ou...]
where the time goes in v3:
time: 50.9 us; the launch traced here: 50.8 us
  Pallas kernels  48.5 us (95%)
  local copies, waits for them, and re-layouts  1.55 us (3%)
  between operations  0.76 us (1%)
    pallas_call x1, Pallas kernels, per_device(): pl.pallas_call(functools.partial(exchange_kernel, facets, side, chans, su...  27.6 us
    pallas_call x1, Pallas kernels, per_device(): pl.pallas_call(functools.partial(grid_kernel, facets, side, subgrids), ou...  16.9 us
    pallas_call x1, Pallas kernels, per_device(): pl.pallas_call(functools.partial(add_kernel, facets), out_shape=shape((2,...  3.97 us

profile of v3, /device:TPU:2, one launch (start us, length us, event | category | flops | bytes accessed | tf_op | source)
XLA Modules:
  0.0 50.8 jit_solution(1144184311458151534)
XLA Ops:
  0.6 0.0 copy-start.2
  0.6 0.0 copy-start.3
  0.7 0.0 copy-start.4
  0.7 0.0 copy-start.1
  0.7 0.0 copy-start
  0.7 0.0 copy-start.5
  0.7 16.9 %grid_and_send.1 = (f32[2048,128]{1,0:T(8,128)S(1)}, s32[16,1,128]{2,1,0:T(1,128)S(1)}, f32[32,256,128]{2,1,0:T(8,128)S(1)}) custom-call(s32[16]{0:T(128)} %cnt.1, s32[16]{0:T(128)} %bitcast.7, s32[16]{0:T(128)} %row_hbm.1, s32[16]{0:T(128)} %col_hbm.1, f32[16,2,512]{2,1,0:T(2,128)} %vis.1, f32[16,2,512]{2,1,0:T(2,128)} %uv.1, ...), custom_call_target="tpu_custom_call" | custom-call | tf_op jit(solution)/shard_map/grid_and_send/pallas_call | solution.py:452
  17.6 4.0 %add_windows.1.canvas = f32[2,32,128,128]{3,2,1,0:T(8,128)S(1)} custom-call(s32[16,1,128]{2,1,0:T(1,128)S(1)} %get-tuple-element.7.meta, f32[2048,128]{1,0:T(8,128)S(1)} %get-tuple-element.8.patches), custom_call_target="tpu_custom_call" | custom-call | tf_op jit(solution)/shard_map/add_windows/pallas_call | solution.py:498
  21.6 0.0 copy-done.2
  21.6 0.0 copy-done.3
  21.6 0.0 copy-done.4
  21.6 0.0 copy-done.1
  21.6 0.0 copy-done
  21.6 0.0 copy-done.5
  21.6 27.6 %reduce_and_return.1 = (f32[512,128]{1,0:T(8,128)S(1)}, f32[16,2,512]{2,1,0:T(2,128)S(1)}) custom-call(s32[16,1,128]{2,1,0:T(1,128)S(1)} %get-tuple-element.7.meta, s32[16]{0:T(128)S(1)} %copy-done.4, s32[16]{0:T(128)S(1)} %bitcast.8, f32[2,32,128,128]{3,2,1,0:T(8,128)S(1)} %add_windows.1.canvas, f32[32,256,128]{2,1,0:T(8,128)S(1)} %get-tuple-element.9.model_rows, ...), custom_call_target="tpu_custom_call" | custom-call | tf_op jit(solution)/shard_map/reduce_and_return/pallas_call | solution.py:509
  49.3 0.1 copy.13
  49.3 0.8 %reshape.11 = f32[1,8,2,4096]{3,2,1,0:T(2,128)} reshape(f32[8,2,32,128]{3,2,1,0:T(8,128)S(1)} %copy.13) | data formatting | bytes 524288 | tf_op jit(solution)/shard_map/reshape | solution.py:540
  50.2 0.6 %copy.15 = f32[16,2,512]{2,1,0:T(2,128)} copy(f32[16,2,512]{2,1,0:T(2,128)S(1)} %get-tuple-element.15) | data formatting | bytes 131072
Async XLA Ops:
  0.6 20.9 %copy-start.2 = (bf16[128,128]{1,0:T(8,128)(2,1)S(1)}, bf16[128,128]{1,0:T(8,128)(2,1)}, u32[]{:S(2)}) copy-start(bf16[128,128]{1,0:T(8,128)(2,1)} %constant.11.clone.right_i) | copy-start | bytes 98308
  0.6 20.9 %copy-start.3 = (bf16[64,128]{1,0:T(8,128)(2,1)S(1)}, bf16[64,128]{1,0:T(8,128)(2,1)}, u32[]{:S(2)}) copy-start(bf16[64,128]{1,0:T(8,128)(2,1)} %constant.10.clone.left_i) | copy-start | bytes 49156
  0.7 20.9 %copy-start.4 = (s32[16]{0:T(128)S(1)}, s32[16]{0:T(128)}, u32[]{:S(2)}) copy-start(s32[16]{0:T(128)} %cnt.1) | copy-start | bytes 196
  0.7 20.9 %copy-start.1 = (f32[16,2,512]{2,1,0:T(2,128)S(1)}, f32[16,2,512]{2,1,0:T(2,128)}, u32[]{:S(2)}) copy-start(f32[16,2,512]{2,1,0:T(2,128)} %uv.1) | copy-start | bytes 196612
  0.7 20.9 %copy-start = (f32[16,2,512]{2,1,0:T(2,128)S(1)}, f32[16,2,512]{2,1,0:T(2,128)}, u32[]{:S(2)}) copy-start(f32[16,2,512]{2,1,0:T(2,128)} %vis.1) | copy-start | bytes 196612
  0.7 20.9 %copy-start.5 = (s32[16,1]{0,1:T(1,128)S(1)}, s32[16,1]{0,1:T(1,128)}, u32[]{:S(2)}) copy-start(s32[16,1]{0,1:T(1,128)} %param.14) | copy-start | bytes 196

commit v4 on v3

--- a/solution.py
+++ b/solution.py
@@ -34,10 +34,21 @@
     return left_forward, right_forward, left_inverse, right_inverse
 
 
+ROOT = math.sqrt(math.log2(math.e))
+
+
+def scaled_square(coords):
+    pixels = lax.broadcasted_iota(jnp.int32, (SUB, NV), 0).astype(jnp.float32) * ROOT
+    delta = pixels - coords * ROOT
+    return delta * delta
+
+
 def kernel_of(coords):
-    pixels = lax.broadcasted_iota(jnp.int32, (SUB, NV), 0).astype(jnp.float32)
-    delta = pixels - coords
-    return jnp.exp(-(delta * delta))
+    return jnp.exp2(-scaled_square(coords))
+
+
+def kernel_low(coords):
+    return jnp.exp2(-(scaled_square(coords).astype(jnp.bfloat16)))
 
 
 def live_row(count):
@@ -45,11 +56,15 @@
     return (lane < count).astype(jnp.float32)
 
 
+def facet_order(side):
+    steps = [(dx, dy) for dx in range(side) for dy in range(side)]
+    return sorted(steps, key=lambda d: (sum(min(n, side - n) for n in d), d))
+
+
 def facet_steps(me, side):
     x, y = me // side, lax.rem(me, side)
     targets, sources = [], []
-    for step in range(1, side * side):
-        dx, dy = step // side, step % side
+    for dx, dy in facet_order(side)[1:]:
         targets.append(lax.rem(x + dx, side) * side + lax.rem(y + dy, side))
         sources.append(lax.rem(x + side - dx, side) * side + lax.rem(y + side - dy, side))
     return targets, sources
@@ -68,23 +83,22 @@
 
 
 def gridded(lines):
-    ku = kernel_of(lines[2:3]).astype(jnp.bfloat16)
-    kv = kernel_of(lines[3:4])
-    spread = jnp.concatenate(
-        [(lines[0:1] * kv).astype(jnp.bfloat16), (lines[1:2] * kv).astype(jnp.bfloat16)], 0
-    )
+    ku = kernel_low(lines[2:3])
+    kv = kernel_low(lines[3:4])
+    weighted = lines[0:2].astype(jnp.bfloat16)
+    spread = jnp.concatenate([weighted[0:1] * kv, weighted[1:2] * kv], 0)
     return lax.dot_general(
         ku, spread, (((1,), (1,)), ((), ())), preferred_element_type=jnp.float32
     ).astype(jnp.bfloat16)
 
 
-GROUP = 2
+GROUP = 4
 
 
 def grid_kernel(
     facets, side, subgrids,
     cnt_hbm, fid_hbm, row_hbm, col_hbm, vis_hbm, uv_hbm, model, left_hbm, right_hbm,
-    patches, meta_in, model_rows,
+    patches, meta_in, model_rows, canvas,
     cnt, fid, row, col, vis, uv, left_f, right_f, raw, lines_send, lines_in, meta_send, first, last,
     in_sem, raw_sem, send_sem, recv_sem, meta_send_sem, meta_recv_sem, own_sem,
 ):
@@ -151,22 +165,18 @@
     lax.fori_loop(0, facets, pack, 0)
 
     pl.semaphore_wait(barrier, facets - 1)
-    copies = [None]
-    metas = []
-    for step, peer in enumerate(targets, 1):
-        pair = []
-        for src, dst, ssem, rsem in (
-            (meta_send, meta_in, meta_send_sem, meta_recv_sem),
-            (lines_send, lines_in, send_sem, recv_sem),
+    copies = [None] * facets
+    metas = [None] * facets
+    for step in range(facets - 1, 0, -1):
+        for src, dst, ssem, rsem, started in (
+            (meta_send, meta_in, meta_send_sem, meta_recv_sem, metas),
+            (lines_send, lines_in, send_sem, recv_sem, copies),
         ):
-            copy = pltpu.make_async_remote_copy(
-                src_ref=src.at[peer], dst_ref=dst.at[step], send_sem=ssem.at[step],
-                recv_sem=rsem.at[step], device_id={"facet": peer},
+            started[step] = pltpu.make_async_remote_copy(
+                src_ref=src.at[targets[step - 1]], dst_ref=dst.at[step], send_sem=ssem.at[step],
+                recv_sem=rsem.at[step], device_id={"facet": targets[step - 1]},
             )
-            copy.start()
-            pair.append(copy)
-        metas.append(pair[0])
-        copies.append(pair[1])
+            started[step].start()
     own = pltpu.make_async_copy(lines_send.at[me], lines_in.at[0], own_sem.at[0])
     own_meta = pltpu.make_async_copy(meta_send.at[me], meta_in.at[0], own_sem.at[1])
     own.start()
@@ -177,9 +187,14 @@
     def widen(tile, carry):
         model_copy(tile).wait()
         model_rows[tile] = rows_view[tile].astype(jnp.float32)
+        canvas[0, tile] = zero
+        canvas[1, tile] = zero
         return carry
 
+    zero = jnp.zeros((F_ROWS, LANES), jnp.float32)
     lax.fori_loop(0, TILES, widen, 0)
+    canvas[0, TILES] = zero
+    canvas[1, TILES] = zero
 
     own.wait()
     own_meta.wait()
@@ -198,59 +213,51 @@
         patches[pl.ds(begin * SLOTS * SUB, GROUP * SLOTS * SUB), :] = out
     for copy in copies[1:]:
         copy.wait_send()
-    for copy in metas:
+    for copy in metas[1:]:
         copy.wait()
 
 
-def add_kernel(facets, meta, patches, canvas):
+def add_kernel(facets, meta, patches, _, canvas):
     lane = lax.broadcasted_iota(jnp.int32, (SUB, LANES), 1)
-    zero = jnp.zeros((F_ROWS, LANES), jnp.float32)
-
-    def clear(tile, carry):
-        canvas[0, tile] = zero
-        canvas[1, tile] = zero
-        return carry
-
-    lax.fori_loop(0, TILES, clear, 0)
 
     def add(step, carry):
         for slot in range(SLOTS):
-            valid = meta[step, 0, 3 * slot]
-
-            @pl.when(valid > 0)
-            def _():
-                top = meta[step, 0, 3 * slot + 1]
-                col = meta[step, 0, 3 * slot + 2]
-                tile, shift = col // LANES, lax.rem(col, LANES)
-                patch = patches[pl.ds(pl.multiple_of((step * 2 + slot) * SUB, SUB), SUB), :]
-                inside = (lane >= shift) & (lane < shift + SUB)
-                at = pl.ds(top, SUB)
-                turned = (
-                    pltpu.roll(patch, shift, 1),
-                    pltpu.roll(patch, lax.rem(shift + SUB, LANES), 1),
+            valid = meta[step, 0, 3 * slot] > 0
+            top = meta[step, 0, 3 * slot + 1]
+            col = meta[step, 0, 3 * slot + 2]
+            tile, shift = col // LANES, lax.rem(col, LANES)
+            low = jnp.where(valid, shift, LANES)
+            high = jnp.where(valid, shift - SUB, 0)
+            patch = patches[pl.ds(pl.multiple_of((step * 2 + slot) * SUB, SUB), SUB), :]
+            inside = (lane >= low) & (lane < shift + SUB)
+            beyond = lane < high
+            at = pl.ds(top, SUB)
+            spots = [(part, tile + next_tile) for part in range(2) for next_tile in range(2)]
+            before = [canvas[part, spot, at, :] for part, spot in spots]
+            turned = (
+                pltpu.roll(patch, shift, 1),
+                pltpu.roll(patch, lax.rem(shift + SUB, LANES), 1),
+            )
+            for i, (part, spot) in enumerate(spots):
+                canvas[part, spot, at, :] = before[i] + jnp.where(
+                    beyond if i % 2 else inside, turned[part], 0.0
                 )
-                for part in range(2):
-                    canvas[part, tile, at, :] += jnp.where(inside, turned[part], 0.0)
-
-                @pl.when(shift > SUB)
-                def _():
-                    beyond = lane < shift - SUB
-                    for part in range(2):
-                        canvas[part, tile + 1, at, :] += jnp.where(beyond, turned[part], 0.0)
-
         return carry
 
-    lax.fori_loop(0, facets, add, 0)
+    lax.fori_loop(0, facets, add, 0, unroll=2)
 
 
 PIECES = 4
+PICKS = 2
+DEGRIDS = 2
+EARLY = 3
 
 
 def exchange_kernel(
     facets, side, chans, subgrids,
     meta, cnt, fid, canvas, model_rows, vis, uv, left_i, right_i,
     total, residual,
-    half_buf, pair_buf, send_buf, recv_buf, halves, back, returned, place,
+    half_buf, pair_buf, send_buf, recv_buf, back, returned, place,
     pair_send, pair_recv, ring_send, ring_recv, back_send, back_recv, own_sem,
 ):
     chips = chans // 2
@@ -269,44 +276,43 @@
 
     lane = lax.broadcasted_iota(jnp.int32, (SUB, LANES), 1)
 
-    def pick(facet, carry):
-        picked = []
-        for slot in range(SLOTS):
-            top = meta[facet, 0, 3 * slot + 1]
-            col = meta[facet, 0, 3 * slot + 2]
-            tile, shift = col // LANES, lax.rem(col, LANES)
-            after = jnp.minimum(tile + 1, TILES - 1)
-            parts = [
-                jnp.where(
-                    lane >= shift,
-                    model_rows[tile, pl.ds(2 * top + part, SUB, stride=2), :],
-                    model_rows[after, pl.ds(2 * top + part, SUB, stride=2), :],
-                )
-                for part in range(2)
-            ]
-            re = pltpu.roll(parts[0], lax.rem(LANES - shift, LANES), 1)
-            im = pltpu.roll(parts[1], lax.rem(LANES + SUB - shift, LANES), 1)
-            picked.append(jnp.where(lane < SUB, re, im).astype(jnp.bfloat16))
-        out = left_pair(left_i[...], picked[0], picked[1])
-        halves[pl.ds(pl.multiple_of(facet * 2 * SUB, 2 * SUB), SUB), :] = out[:, :LANES]
-        halves[pl.ds(pl.multiple_of(facet * 2 * SUB + SUB, SUB), SUB), :] = out[:, LANES:]
-        return carry
-
-    def inverse_right(block, carry):
-        at = pl.ds(pl.multiple_of(block * 256, 256), 256)
-        out = jnp.dot(halves[at, :], right_i[...], preferred_element_type=jnp.float32)
-        out = out.astype(jnp.bfloat16)
-        for i in range(2):
+    def picked(step, slot):
+        top = meta[step, 0, 3 * slot + 1]
+        col = meta[step, 0, 3 * slot + 2]
+        tile, shift = col // LANES, lax.rem(col, LANES)
+        after = jnp.minimum(tile + 1, TILES - 1)
+        parts = [
+            jnp.where(
+                lane >= shift,
+                model_rows[tile, pl.ds(2 * top + part, SUB, stride=2), :],
+                model_rows[after, pl.ds(2 * top + part, SUB, stride=2), :],
+            )
+            for part in range(2)
+        ]
+        re = pltpu.roll(parts[0], lax.rem(LANES - shift, LANES), 1)
+        im = pltpu.roll(parts[1], lax.rem(LANES + SUB - shift, LANES), 1)
+        return jnp.where(lane < SUB, re, im).astype(jnp.bfloat16)
+
+    def pick(begin):
+        halves = []
+        for step in range(begin, begin + PICKS):
+            out = left_pair(left_i[...], picked(step, 0), picked(step, 1))
+            halves += [out[:, :LANES], out[:, LANES:]]
+        out = jnp.dot(
+            jnp.concatenate(halves, 0), right_i[...], preferred_element_type=jnp.float32
+        ).astype(jnp.bfloat16)
+        for i in range(PICKS):
             for slot in range(SLOTS):
-                begin = (2 * i + slot) * SUB
-                back[2 * block + i, slot] = out[begin : begin + SUB]
-        return carry
+                at = (2 * i + slot) * SUB
+                back[begin + i, slot] = out[at : at + SUB]
 
     half = chips // 2
     offsets = [half]
     for d in range(half - 1, 0, -1):
         offsets += [d, chips - d]
     offsets += [0]
+
+    work = [functools.partial(pick, begin) for begin in range(facets - PICKS, -1, -PICKS)]
 
     def chan_rows(offset, which):
         there = lax.rem(z + offset, chips)
@@ -321,6 +327,8 @@
         return carry
 
     lax.fori_loop(0, TILES // 2, narrow, 0)
+    for _ in range(EARLY):
+        work.pop(0)()
     pl.semaphore_wait(barrier, 3 + facets - 1)
 
     pair_copy = {}
@@ -331,8 +339,6 @@
         )
         copy.start()
         pair_copy[offset] = copy
-
-    lax.fori_loop(0, facets // 2, pick, 0, unroll=2)
 
     depth = half_buf.shape[1] // PIECES
     arrived = set()
@@ -352,7 +358,8 @@
 
     ring = {}
 
-    def ring_step(step):
+    def ring_step(step, every):
+        done = 0
         for piece in range(PIECES):
             for way in range(2):
                 count = length(piece, way)
@@ -373,58 +380,75 @@
                 )
                 copy.start()
                 ring[way, piece, step] = copy
-
-    def degrid(s, carry):
-        image = returned[place[s], place[subgrids + s]]
-        ku = kernel_of(uv[s, pl.ds(0, 1), :]).astype(jnp.bfloat16)
-        weight = kernel_of(uv[s, pl.ds(1, 1), :])
-        inner = lax.dot_general(
-            image, ku, (((0,), (0,)), ((), ())), preferred_element_type=jnp.float32
-        )
-        live = live_row(cnt[s])
-        for part in range(2):
-            predicted = jnp.sum(inner[part * SUB : (part + 1) * SUB] * weight, 0, keepdims=True)
-            residual[s, pl.ds(part, 1), :] = (vis[s, pl.ds(part, 1), :] - predicted) * live
-        return carry
-
-    ring_step(0)
-    lax.fori_loop(facets // 2, facets, pick, 0, unroll=2)
-    lax.fori_loop(0, facets * SLOTS * SUB // 256, inverse_right, 0, unroll=2)
+                done += 1
+                if done % every == 0 and work:
+                    work.pop(0)()
+
+    def degrid(begin):
+        for s in range(begin, begin + DEGRIDS):
+            image = returned[place[s], place[subgrids + s]]
+            ku = kernel_low(uv[s, pl.ds(0, 1), :])
+            weight = kernel_of(uv[s, pl.ds(1, 1), :])
+            inner = lax.dot_general(
+                image, ku, (((0,), (0,)), ((), ())), preferred_element_type=jnp.float32
+            )
+            live = live_row(cnt[s])
+            for part in range(2):
+                predicted = jnp.sum(inner[part * SUB : (part + 1) * SUB] * weight, 0, keepdims=True)
+                residual[s, pl.ds(part, 1), :] = (vis[s, pl.ds(part, 1), :] - predicted) * live
+
     back_copy = []
-    for step in range(1, facets):
-        copy = pltpu.make_async_remote_copy(
-            src_ref=back.at[step], dst_ref=returned.at[step],
-            send_sem=back_send.at[step], recv_sem=back_recv.at[step],
-            device_id={"facet": sources[step - 1]},
-        )
-        copy.start()
-        back_copy.append(copy)
-    own = pltpu.make_async_copy(back.at[0], returned.at[0], own_sem)
-    own.start()
-    ring_step(1)
-    ids = [fid[s] for s in range(subgrids)]
-    x, y = me_f // side, lax.rem(me_f, side)
-    for s in range(subgrids):
-        before = jnp.int32(0)
-        for other in range(s):
-            before = jnp.where(ids[other] == ids[s], 1, before)
-        there_x, there_y = ids[s] // side, lax.rem(ids[s], side)
-        place[s] = lax.rem(there_x + side - x, side) * side + lax.rem(there_y + side - y, side)
-        place[subgrids + s] = before
-    ring_step(2)
+
+    def send_back():
+        for step in range(facets - 1, 0, -1):
+            copy = pltpu.make_async_remote_copy(
+                src_ref=back.at[step], dst_ref=returned.at[step],
+                send_sem=back_send.at[step], recv_sem=back_recv.at[step],
+                device_id={"facet": sources[step - 1]},
+            )
+            copy.start()
+            back_copy.append(copy)
+        own = pltpu.make_async_copy(back.at[0], returned.at[0], own_sem)
+        own.start()
+        back_copy.append(own)
+
+    def locate():
+        ids = [fid[s] for s in range(subgrids)]
+        x, y = me_f // side, lax.rem(me_f, side)
+        codes = []
+        for s in range(subgrids):
+            before = jnp.int32(0)
+            for other in range(s):
+                before = jnp.where(ids[other] == ids[s], 1, before)
+            there_x, there_y = ids[s] // side, lax.rem(ids[s], side)
+            code = lax.rem(there_x + side - x, side) * side + lax.rem(there_y + side - y, side)
+            where = jnp.int32(0)
+            for step, known in enumerate(facet_order(side)):
+                where = jnp.where(code == known[0] * side + known[1], step, where)
+            place[s] = where
+            place[subgrids + s] = before
+
+    work += [send_back, locate]
+    ring_step(0, 1)
+    while work:
+        work.pop(0)()
+    ring_step(1, 1)
+    ring_step(2, 1)
     for copy in back_copy:
         copy.wait()
-    own.wait()
-    lax.fori_loop(0, subgrids // 2, degrid, 0, unroll=2)
-    ring_step(3)
-    lax.fori_loop(subgrids // 2, subgrids, degrid, 0, unroll=2)
+    work += [functools.partial(degrid, s) for s in range(0, subgrids, DEGRIDS)]
+    ring_step(half - 1, 1)
     for piece in range(PIECES):
+        if work:
+            work.pop(0)()
         value = mine(0, piece)
         for way in range(2):
             step = length(piece, way) - 1
             ring[way, piece, step].wait_recv()
             value = value + recv_buf[(way * PIECES + piece) * half + step].astype(jnp.float32)
         total[pl.ds(piece * depth, depth), :] = value
+    while work:
+        work.pop(0)()
     for copy in pair_copy.values():
         copy.wait_send()
     for copy in ring.values():
@@ -449,15 +473,16 @@
     ids = subgrid_facet[:, 0]
 
     lines = (facets, SLOTS * 4, NV)
-    patches, meta, model_rows = pl.pallas_call(
+    patches, meta, model_rows, zeros = pl.pallas_call(
         functools.partial(grid_kernel, facets, side, subgrids),
         out_shape=(
             shape((facets * SLOTS * SUB, LANES), jnp.float32),
             shape((facets, 1, LANES), jnp.int32),
             shape((TILES, 2 * F_ROWS, LANES), jnp.float32),
+            shape((2, TILES + 1, F_ROWS, LANES), jnp.float32),
         ),
         in_specs=[HBM] * 9,
-        out_specs=(VMEM,) * 3,
+        out_specs=(VMEM,) * 4,
         scratch_shapes=[
             pltpu.SMEM((subgrids,), jnp.int32),
             pltpu.SMEM((subgrids,), jnp.int32),
@@ -497,12 +522,13 @@
 
     canvas = pl.pallas_call(
         functools.partial(add_kernel, facets),
-        out_shape=shape((2, TILES, F_ROWS, LANES), jnp.float32),
-        in_specs=[SMEM, VMEM],
+        out_shape=shape((2, TILES + 1, F_ROWS, LANES), jnp.float32),
+        in_specs=[SMEM, VMEM, VMEM],
         out_specs=VMEM,
+        input_output_aliases={2: 0},
         compiler_params=pltpu.CompilerParams(vmem_limit_bytes=16 << 20),
         name="add_windows",
-    )(meta, patches)
+    )(meta, patches, zeros)
 
     depth = 2 * TILES * rows // PIECES
     links = 2 * PIECES * (chips // 2)
@@ -519,7 +545,6 @@
             pltpu.VMEM((chips, 2 * TILES * rows, LANES), jnp.bfloat16),
             pltpu.VMEM((links, depth, LANES), jnp.bfloat16),
             pltpu.VMEM((links, depth, LANES), jnp.bfloat16),
-            pltpu.VMEM((facets * SLOTS * SUB, LANES), jnp.bfloat16),
             pltpu.VMEM((facets, SLOTS, SUB, LANES), jnp.bfloat16),
             pltpu.VMEM((facets, SLOTS, SUB, LANES), jnp.bfloat16),
             pltpu.SMEM((2 * subgrids,), jnp.int32),

time: 50.9 us -> 46.9 us (0.921)
  the two profiles are of different devices: /device:TPU:2 before, /device:TPU:1 now
where the time goes in v4:
time: 46.9 us; the launch traced here: 46.7 us
  Pallas kernels  44.4 us (95%)
  local copies, waits for them, and re-layouts  1.56 us (3%)
  between operations  0.76 us (2%)
    pallas_call x1, Pallas kernels, per_device(): pl.pallas_call(functools.partial(exchange_kernel, facets, side, chans, su...  25 us
    pallas_call x1, Pallas kernels, per_device(): pl.pallas_call(functools.partial(grid_kernel, facets, side, subgrids), ou...  17.6 us
    pallas_call x1, Pallas kernels, per_device(): pl.pallas_call(functools.partial(add_kernel, facets), out_shape=shape((2,...  1.8 us

profile of v4, /device:TPU:1, one launch (start us, length us, event | category | flops | bytes accessed | tf_op | source)
XLA Modules:
  0.0 46.7 jit_solution(11072182992640638390)
XLA Ops:
  0.6 17.6 %grid_and_send.1 = (f32[2048,128]{1,0:T(8,128)S(1)}, s32[16,1,128]{2,1,0:T(1,128)S(1)}, f32[32,256,128]{2,1,0:T(8,128)S(1)}, f32[2,33,128,128]{3,2,1,0:T(8,128)S(1)}) custom-call(s32[16]{0:T(128)} %cnt.1, s32[16]{0:T(128)} %bitcast.7, s32[16]{0:T(128)} %row_hbm.1, s32[16]{0:T(128)} %col_hbm.1, f32[16,2,512]{2,1,0:T(2,128)} %vis.1, f32[16,2,512]{2,1,0:T(2,128)} %uv.1, ...), custom_call_target="tpu_custom_call" | custom-call | tf_op jit(solution)/shard_map/grid_and_send/pallas_call | solution.py:476
  18.2 0.0 copy-start
  18.2 0.0 copy-start.1
  18.2 0.0 copy-start.2
  18.3 0.0 copy-start.3
  18.3 0.0 copy-start.4
  18.3 0.0 copy-start.5
  18.3 1.8 %add_windows.1.canvas = f32[2,33,128,128]{3,2,1,0:T(8,128)S(1)} custom-call(s32[16,1,128]{2,1,0:T(1,128)S(1)} %get-tuple-element.8.meta, f32[2048,128]{1,0:T(8,128)S(1)} %get-tuple-element.9.patches, f32[2,33,128,128]{3,2,1,0:T(8,128)S(1)} %get-tuple-element.10._), custom_call_target="tpu_custom_call", output_to_operand_aliasing={{}: (2, {})} | custom-call | tf_op jit(solution)/shard_map/add_windows/pallas_call | solution.py:523
  20.1 0.0 copy-done
  20.1 0.0 copy-done.1
  20.1 0.0 copy-done.2
  20.1 0.0 copy-done.3
  20.1 0.0 copy-done.4
  20.2 0.0 copy-done.5
  20.2 25.0 %reduce_and_return.1 = (f32[512,128]{1,0:T(8,128)S(1)}, f32[16,2,512]{2,1,0:T(2,128)S(1)}) custom-call(s32[16,1,128]{2,1,0:T(1,128)S(1)} %get-tuple-element.8.meta, s32[16]{0:T(128)S(1)} %copy-done.4, s32[16]{0:T(128)S(1)} %bitcast.8, f32[2,33,128,128]{3,2,1,0:T(8,128)S(1)} %add_windows.1.canvas, f32[32,256,128]{2,1,0:T(8,128)S(1)} %get-tuple-element.11.model_rows, ...), custom_call_target="tpu_custom_call" | custom-call | tf_op jit(solution)/shard_map/reduce_and_return/pallas_call | solution.py:535
  45.2 0.1 copy.14
  45.3 0.8 %reshape.11 = f32[1,8,2,4096]{3,2,1,0:T(2,128)} reshape(f32[8,2,32,128]{3,2,1,0:T(8,128)S(1)} %copy.14) | data formatting | bytes 524288 | tf_op jit(solution)/shard_map/reshape | solution.py:565
  46.1 0.6 %copy.17 = f32[16,2,512]{2,1,0:T(2,128)} copy(f32[16,2,512]{2,1,0:T(2,128)S(1)} %get-tuple-element.17) | data formatting | bytes 131072
Async XLA Ops:
  18.2 1.9 %copy-start = (f32[16,2,512]{2,1,0:T(2,128)S(1)}, f32[16,2,512]{2,1,0:T(2,128)}, u32[]{:S(2)}) copy-start(f32[16,2,512]{2,1,0:T(2,128)} %vis.1) | copy-start | bytes 196612
  18.2 1.9 %copy-start.1 = (f32[16,2,512]{2,1,0:T(2,128)S(1)}, f32[16,2,512]{2,1,0:T(2,128)}, u32[]{:S(2)}) copy-start(f32[16,2,512]{2,1,0:T(2,128)} %uv.1) | copy-start | bytes 196612
  18.2 1.9 %copy-start.2 = (bf16[128,128]{1,0:T(8,128)(2,1)S(1)}, bf16[128,128]{1,0:T(8,128)(2,1)}, u32[]{:S(2)}) copy-start(bf16[128,128]{1,0:T(8,128)(2,1)} %constant.11.clone.right_i) | copy-start | bytes 98308
  18.3 1.9 %copy-start.3 = (bf16[64,128]{1,0:T(8,128)(2,1)S(1)}, bf16[64,128]{1,0:T(8,128)(2,1)}, u32[]{:S(2)}) copy-start(bf16[64,128]{1,0:T(8,128)(2,1)} %constant.10.clone.left_i) | copy-start | bytes 49156
  18.3 1.9 %copy-start.4 = (s32[16]{0:T(128)S(1)}, s32[16]{0:T(128)}, u32[]{:S(2)}) copy-start(s32[16]{0:T(128)} %cnt.1) | copy-start | bytes 196
  18.3 1.9 %copy-start.5 = (s32[16,1]{0,1:T(1,128)S(1)}, s32[16,1]{0,1:T(1,128)}, u32[]{:S(2)}) copy-start(s32[16,1]{0,1:T(1,128)} %param.14) | copy-start | bytes 196

commit v5 on v4

--- a/solution.py
+++ b/solution.py
@@ -1,4 +1,5 @@
 import functools
+import itertools
 import math
 
 import jax
@@ -48,7 +49,7 @@
 
 
 def kernel_low(coords):
-    return jnp.exp2(-(scaled_square(coords).astype(jnp.bfloat16)))
+    return kernel_of(coords).astype(jnp.bfloat16)
 
 
 def live_row(count):
@@ -82,25 +83,25 @@
     return out.astype(jnp.bfloat16)
 
 
-def gridded(lines):
-    ku = kernel_low(lines[2:3])
-    kv = kernel_low(lines[3:4])
-    weighted = lines[0:2].astype(jnp.bfloat16)
+def gridded(coords, weighted):
+    ku = kernel_low(coords[0:1])
+    kv = kernel_low(coords[1:2])
     spread = jnp.concatenate([weighted[0:1] * kv, weighted[1:2] * kv], 0)
     return lax.dot_general(
         ku, spread, (((1,), (1,)), ((), ())), preferred_element_type=jnp.float32
     ).astype(jnp.bfloat16)
 
 
-GROUP = 4
+SIZES = (6, 6, 4)
 
 
 def grid_kernel(
     facets, side, subgrids,
     cnt_hbm, fid_hbm, row_hbm, col_hbm, vis_hbm, uv_hbm, model, left_hbm, right_hbm,
     patches, meta_in, model_rows, canvas,
-    cnt, fid, row, col, vis, uv, left_f, right_f, raw, lines_send, lines_in, meta_send, first, last,
-    in_sem, raw_sem, send_sem, recv_sem, meta_send_sem, meta_recv_sem, own_sem,
+    cnt, fid, row, col, vis, uv, left_f, right_f, raw, vis_send, vis_in, uv_send, uv_in, meta_send,
+    grids, halves, first, last,
+    in_sem, raw_sem, send_sem, recv_sem, own_sem,
 ):
     me = lax.axis_index("facet")
     targets, _ = facet_steps(me, side)
@@ -149,9 +150,9 @@
         low, high = first[facet], last[facet]
         one = jnp.minimum(low, subgrids - 1)
         two = jnp.maximum(high, 0)
-        lines_send[facet] = jnp.concatenate(
-            [vis[one] * live_row(cnt[one]), uv[one], vis[two] * live_row(cnt[two]), uv[two]], 0
-        )
+        weighted = [vis[s] * live_row(cnt[s]) for s in (one, two)]
+        vis_send[facet] = jnp.concatenate(weighted, 0).astype(jnp.bfloat16)
+        uv_send[facet] = jnp.concatenate([uv[one], uv[two]], 0)
         values = (
             (high >= 0).astype(jnp.int32), row[one], col[one],
             (high > low).astype(jnp.int32), row[two], col[two],
@@ -165,22 +166,20 @@
     lax.fori_loop(0, facets, pack, 0)
 
     pl.semaphore_wait(barrier, facets - 1)
-    copies = [None] * facets
-    metas = [None] * facets
-    for step in range(facets - 1, 0, -1):
-        for src, dst, ssem, rsem, started in (
-            (meta_send, meta_in, meta_send_sem, meta_recv_sem, metas),
-            (lines_send, lines_in, send_sem, recv_sem, copies),
-        ):
-            started[step] = pltpu.make_async_remote_copy(
-                src_ref=src.at[targets[step - 1]], dst_ref=dst.at[step], send_sem=ssem.at[step],
-                recv_sem=rsem.at[step], device_id={"facet": targets[step - 1]},
-            )
-            started[step].start()
-    own = pltpu.make_async_copy(lines_send.at[me], lines_in.at[0], own_sem.at[0])
-    own_meta = pltpu.make_async_copy(meta_send.at[me], meta_in.at[0], own_sem.at[1])
-    own.start()
-    own_meta.start()
+    moved = ((meta_send, meta_in), (vis_send, vis_in), (uv_send, uv_in))
+    copies = [[] for _ in range(facets)]
+    for step in range(facets - 1, -1, -1):
+        for i, (src, dst) in enumerate(moved):
+            if step > 0:
+                copy = pltpu.make_async_remote_copy(
+                    src_ref=src.at[targets[step - 1]], dst_ref=dst.at[step],
+                    send_sem=send_sem.at[i, step], recv_sem=recv_sem.at[i, step],
+                    device_id={"facet": targets[step - 1]},
+                )
+            else:
+                copy = pltpu.make_async_copy(src.at[me], dst.at[0], own_sem.at[i])
+            copy.start()
+            copies[step].append(copy)
 
     rows_view = raw.reshape(TILES, 2 * F_ROWS, LANES)
 
@@ -196,25 +195,43 @@
     canvas[0, TILES] = zero
     canvas[1, TILES] = zero
 
-    own.wait()
-    own_meta.wait()
-    for begin in range(0, facets, GROUP):
-        halves = []
-        for step in range(begin, begin + GROUP):
-            if step > 0:
-                copies[step].wait_recv()
-        for step in range(begin, begin + GROUP):
-            lines = lines_in[step]
-            out = left_pair(left_f[...], gridded(lines[:4]), gridded(lines[4:]))
-            halves += [out[:, :LANES], out[:, LANES:]]
-        out = jnp.dot(
-            jnp.concatenate(halves, 0), right_f[...], preferred_element_type=jnp.float32
+    def grid_one(step):
+        for slot in range(SLOTS):
+            at = pl.ds(2 * slot, 2)
+            grids[SLOTS * step + slot] = gridded(uv_in[step, at, :], vis_in[step, at, :])
+
+    def left_one(step):
+        out = left_pair(left_f[...], grids[SLOTS * step], grids[SLOTS * step + 1])
+        halves[SLOTS * step] = out[:, :LANES]
+        halves[SLOTS * step + 1] = out[:, LANES:]
+
+    def right_one(step):
+        both = halves[pl.ds(SLOTS * step, SLOTS)].reshape(SLOTS * SUB, LANES)
+        patches[pl.ds(SLOTS * SUB * step, SLOTS * SUB), :] = jnp.dot(
+            both, right_f[...], preferred_element_type=jnp.float32
         )
-        patches[pl.ds(begin * SLOTS * SUB, GROUP * SLOTS * SUB), :] = out
-    for copy in copies[1:]:
-        copy.wait_send()
-    for copy in metas[1:]:
-        copy.wait()
+
+    begins = [0]
+    for size in SIZES:
+        begins.append(begins[-1] + size)
+    groups = [range(a, b) for a, b in zip(begins, begins[1:])]
+    stages = (grid_one, left_one, right_one)
+    for turn in range(len(groups) + len(stages) - 1):
+        if turn < len(groups):
+            for step in groups[turn]:
+                for copy in copies[step]:
+                    copy.wait_recv() if step > 0 else copy.wait()
+        now = []
+        for lag, stage in enumerate(stages):
+            if 0 <= turn - lag < len(groups):
+                now.append([functools.partial(stage, step) for step in groups[turn - lag]])
+        for parts in itertools.zip_longest(*now):
+            for part in reversed(parts):
+                if part is not None:
+                    part()
+    for step in range(1, facets):
+        for copy in copies[step]:
+            copy.wait_send()
 
 
 def add_kernel(facets, meta, patches, _, canvas):
@@ -249,8 +266,8 @@
 
 PIECES = 4
 PICKS = 2
-DEGRIDS = 2
-EARLY = 3
+DEGRIDS = 4
+EARLY = 8
 
 
 def exchange_kernel(
@@ -455,6 +472,18 @@
         copy.wait_send()
 
 
+def output_kernel(rows, total, values, image, residual):
+    def place(tile, carry):
+        at = pl.ds(pl.multiple_of(tile * LANES, LANES), LANES)
+        for part in range(2):
+            begin = pl.multiple_of((part * TILES + tile) * rows, rows)
+            image[0, :, part, at] = total[pl.ds(begin, rows), :]
+        return carry
+
+    lax.fori_loop(0, TILES, place, 0, unroll=4)
+    residual[...] = values[...]
+
+
 VMEM = pl.BlockSpec(memory_space=pltpu.VMEM)
 SMEM = pl.BlockSpec(memory_space=pltpu.SMEM)
 HBM = pl.BlockSpec(memory_space=pltpu.HBM)
@@ -472,7 +501,6 @@
     left_f, right_f, left_i, right_i = (jnp.asarray(table) for table in dft_tables())
     ids = subgrid_facet[:, 0]
 
-    lines = (facets, SLOTS * 4, NV)
     patches, meta, model_rows, zeros = pl.pallas_call(
         functools.partial(grid_kernel, facets, side, subgrids),
         out_shape=(
@@ -493,18 +521,20 @@
             pltpu.VMEM(left_f.shape, jnp.bfloat16),
             pltpu.VMEM(right_f.shape, jnp.bfloat16),
             pltpu.VMEM((TILES, F_ROWS, 2, LANES), jnp.bfloat16),
-            pltpu.VMEM(lines, jnp.float32),
-            pltpu.VMEM(lines, jnp.float32),
+            pltpu.VMEM((facets, 2 * SLOTS, NV), jnp.bfloat16),
+            pltpu.VMEM((facets, 2 * SLOTS, NV), jnp.bfloat16),
+            pltpu.VMEM((facets, 2 * SLOTS, NV), jnp.float32),
+            pltpu.VMEM((facets, 2 * SLOTS, NV), jnp.float32),
             pltpu.VMEM((facets, 1, LANES), jnp.int32),
+            pltpu.VMEM((facets * SLOTS, SUB, LANES), jnp.bfloat16),
+            pltpu.VMEM((facets * SLOTS, SUB, LANES), jnp.bfloat16),
             pltpu.SMEM((facets,), jnp.int32),
             pltpu.SMEM((facets,), jnp.int32),
             pltpu.SemaphoreType.DMA((8,)),
             pltpu.SemaphoreType.DMA((TILES,)),
-            pltpu.SemaphoreType.DMA((facets,)),
-            pltpu.SemaphoreType.DMA((facets,)),
-            pltpu.SemaphoreType.DMA((facets,)),
-            pltpu.SemaphoreType.DMA((facets,)),
-            pltpu.SemaphoreType.DMA((2,)),
+            pltpu.SemaphoreType.DMA((3, facets)),
+            pltpu.SemaphoreType.DMA((3, facets)),
+            pltpu.SemaphoreType.DMA((3,)),
         ],
         compiler_params=pltpu.CompilerParams(
             collective_id=0, has_side_effects=True, vmem_limit_bytes=16 << 20
@@ -562,7 +592,17 @@
         name="reduce_and_return",
     )(meta, vis_count, ids, canvas, model_rows, visibility, uv_coords, left_i, right_i)
 
-    image = total.reshape(2, TILES, rows, LANES).transpose(2, 0, 1, 3).reshape(1, rows, 2, FACET)
+    image, residual = pl.pallas_call(
+        functools.partial(output_kernel, rows),
+        out_shape=(
+            shape((1, rows, 2, FACET), jnp.float32),
+            shape(visibility.shape, jnp.float32),
+        ),
+        in_specs=[VMEM] * 2,
+        out_specs=(VMEM,) * 2,
+        compiler_params=pltpu.CompilerParams(vmem_limit_bytes=8 << 20),
+        name="outputs",
+    )(total, residual)
     return image, residual
 
 

time: 46.9 us -> 41.8 us (0.89)
  the two profiles are of different devices: /device:TPU:1 before, /device:TPU:2 now
where the time goes in v5:
time: 41.8 us; the launch traced here: 41 us
  Pallas kernels  40.2 us (96%)
  between operations  0.75 us (2%)
    pallas_call x1, Pallas kernels, per_device(): pl.pallas_call(functools.partial(exchange_kernel, facets, side, chans, su...  24.2 us
    pallas_call x1, Pallas kernels, per_device(): pl.pallas_call(functools.partial(grid_kernel, facets, side, subgrids), ou...  13.2 us
    pallas_call x1, Pallas kernels, per_device(): pl.pallas_call(functools.partial(add_kernel, facets), out_shape=shape((2,...  1.8 us
    pallas_call x1, Pallas kernels, per_device(): pl.pallas_call(functools.partial(output_kernel, rows), out_shape=(shape((...  0.98 us

profile of v5, /device:TPU:2, one launch (start us, length us, event | category | flops | bytes accessed | tf_op | source)
XLA Modules:
  0.0 41.0 jit_solution(13148195375406856370)
XLA Ops:
  0.6 13.2 %grid_and_send.1 = (f32[2048,128]{1,0:T(8,128)S(1)}, s32[16,1,128]{2,1,0:T(1,128)S(1)}, f32[32,256,128]{2,1,0:T(8,128)S(1)}, f32[2,33,128,128]{3,2,1,0:T(8,128)S(1)}) custom-call(s32[16]{0:T(128)} %cnt.1, s32[16]{0:T(128)} %bitcast.1, s32[16]{0:T(128)} %row_hbm.1, s32[16]{0:T(128)} %col_hbm.1, f32[16,2,512]{2,1,0:T(2,128)} %vis.1, f32[16,2,512]{2,1,0:T(2,128)} %uv.1, ...), custom_call_target="tpu_custom_call" | custom-call | tf_op jit(solution)/shard_map/grid_and_send/pallas_call | solution.py:504
  13.9 0.0 copy-start
  13.9 0.0 copy-start.1
  13.9 0.0 copy-start.2
  13.9 0.0 copy-start.3
  13.9 0.0 copy-start.4
  13.9 0.0 copy-start.5
  14.0 1.8 %add_windows.1.canvas = f32[2,33,128,128]{3,2,1,0:T(8,128)S(1)} custom-call(s32[16,1,128]{2,1,0:T(1,128)S(1)} %get-tuple-element.8.meta, f32[2048,128]{1,0:T(8,128)S(1)} %get-tuple-element.9.patches, f32[2,33,128,128]{3,2,1,0:T(8,128)S(1)} %get-tuple-element.10._), custom_call_target="tpu_custom_call", output_to_operand_aliasing={{}: (2, {})} | custom-call | tf_op jit(solution)/shard_map/add_windows/pallas_call | solution.py:553
  15.8 0.0 copy-done
  15.8 0.0 copy-done.1
  15.8 0.0 copy-done.2
  15.8 0.0 copy-done.3
  15.8 0.0 copy-done.4
  15.8 0.0 copy-done.5
  15.8 24.2 %reduce_and_return.1 = (f32[512,128]{1,0:T(8,128)S(1)}, f32[16,2,512]{2,1,0:T(2,128)S(1)}) custom-call(s32[16,1,128]{2,1,0:T(1,128)S(1)} %get-tuple-element.8.meta, s32[16]{0:T(128)S(1)} %copy-done.4, s32[16]{0:T(128)S(1)} %bitcast.2, f32[2,33,128,128]{3,2,1,0:T(8,128)S(1)} %add_windows.1.canvas, f32[32,256,128]{2,1,0:T(8,128)S(1)} %get-tuple-element.11.model_rows, ...), custom_call_target="tpu_custom_call" | custom-call | tf_op jit(solution)/shard_map/reduce_and_return/pallas_call | solution.py:565
  40.0 1.0 %outputs.1 = (f32[1,8,2,4096]{3,2,1,0:T(2,128)}, f32[16,2,512]{2,1,0:T(2,128)}) custom-call(f32[512,128]{1,0:T(8,128)S(1)} %get-tuple-element.12.total, f32[16,2,512]{2,1,0:T(2,128)S(1)} %get-tuple-element.13.values), custom_call_target="tpu_custom_call" | custom-call | tf_op jit(solution)/shard_map/outputs/pallas_call | solution.py:595
Async XLA Ops:
  13.9 1.9 %copy-start = (f32[16,2,512]{2,1,0:T(2,128)S(1)}, f32[16,2,512]{2,1,0:T(2,128)}, u32[]{:S(2)}) copy-start(f32[16,2,512]{2,1,0:T(2,128)} %vis.1) | copy-start | bytes 196612
  13.9 1.9 %copy-start.1 = (f32[16,2,512]{2,1,0:T(2,128)S(1)}, f32[16,2,512]{2,1,0:T(2,128)}, u32[]{:S(2)}) copy-start(f32[16,2,512]{2,1,0:T(2,128)} %uv.1) | copy-start | bytes 196612
  13.9 1.9 %copy-start.2 = (bf16[128,128]{1,0:T(8,128)(2,1)S(1)}, bf16[128,128]{1,0:T(8,128)(2,1)}, u32[]{:S(2)}) copy-start(bf16[128,128]{1,0:T(8,128)(2,1)} %constant.11.clone.right_i) | copy-start | bytes 98308
  13.9 1.9 %copy-start.3 = (bf16[64,128]{1,0:T(8,128)(2,1)S(1)}, bf16[64,128]{1,0:T(8,128)(2,1)}, u32[]{:S(2)}) copy-start(bf16[64,128]{1,0:T(8,128)(2,1)} %constant.10.clone.left_i) | copy-start | bytes 49156
  13.9 1.9 %copy-start.4 = (s32[16]{0:T(128)S(1)}, s32[16]{0:T(128)}, u32[]{:S(2)}) copy-start(s32[16]{0:T(128)} %cnt.1) | copy-start | bytes 196
  13.9 1.9 %copy-start.5 = (s32[16,1]{0,1:T(1,128)S(1)}, s32[16,1]{0,1:T(1,128)}, u32[]{:S(2)}) copy-start(s32[16,1]{0,1:T(1,128)} %param.14) | copy-start | bytes 196

commit v6 on v5

--- a/solution.py
+++ b/solution.py
@@ -267,7 +267,6 @@
 PIECES = 4
 PICKS = 2
 DEGRIDS = 4
-EARLY = 8
 
 
 def exchange_kernel(
@@ -275,7 +274,7 @@
     meta, cnt, fid, canvas, model_rows, vis, uv, left_i, right_i,
     total, residual,
     half_buf, pair_buf, send_buf, recv_buf, back, returned, place,
-    pair_send, pair_recv, ring_send, ring_recv, back_send, back_recv, own_sem,
+    pair_send, pair_recv, ring_send, ring_recv, back_send, back_recv, own_sem, near_sem, far_sem,
 ):
     chips = chans // 2
     me_f, me_c = lax.axis_index("facet"), lax.axis_index("chan")
@@ -284,11 +283,14 @@
     right = lax.rem(z + 1, chips) * 2 + core
     left = lax.rem(z + chips - 1, chips) * 2 + core
     targets, sources = facet_steps(me_f, side)
+    hops = [sum(min(n, side - n) for n in d) for d in facet_order(side)][1:]
+    near = [peer for peer, hop in zip(targets, hops) if hop == 1]
+    middle = [peer for peer, hop in zip(targets, hops) if hop == 2]
     rows = F_ROWS // chans
     barrier = pltpu.get_barrier_semaphore()
     for peer in (partner, right, left):
         pl.semaphore_signal(barrier, inc=1, device_id={"chan": peer})
-    for peer in targets:
+    for peer in near:
         pl.semaphore_signal(barrier, inc=1, device_id={"facet": peer})
 
     lane = lax.broadcasted_iota(jnp.int32, (SUB, LANES), 1)
@@ -324,10 +326,20 @@
                 back[begin + i, slot] = out[at : at + SUB]
 
     half = chips // 2
-    offsets = [half]
-    for d in range(half - 1, 0, -1):
-        offsets += [d, chips - d]
-    offsets += [0]
+    depth = half_buf.shape[1] // PIECES
+
+    def length(piece, way):
+        return half - (piece + way) % 2
+
+    needed = []
+    for step in range(half):
+        for piece in range(PIECES):
+            for way in range(2):
+                distance = length(piece, way) - step
+                need = (distance % chips if way == 0 else (chips - distance) % chips, piece)
+                if distance > 0 and need not in needed:
+                    needed.append(need)
+    needed += [(0, piece) for piece in range(PIECES)]
 
     work = [functools.partial(pick, begin) for begin in range(facets - PICKS, -1, -PICKS)]
 
@@ -344,39 +356,35 @@
         return carry
 
     lax.fori_loop(0, TILES // 2, narrow, 0)
-    for _ in range(EARLY):
-        work.pop(0)()
-    pl.semaphore_wait(barrier, 3 + facets - 1)
+    pl.semaphore_wait(barrier, 3 + len(near))
+    for peer in near:
+        pl.semaphore_signal(near_sem, inc=1, device_id={"facet": peer})
 
     pair_copy = {}
-    for offset in offsets:
+    for i, (offset, piece) in enumerate(needed):
+        at = pl.ds(piece * depth, depth)
         copy = pltpu.make_async_remote_copy(
-            src_ref=half_buf.at[offset], dst_ref=pair_buf.at[offset],
-            send_sem=pair_send.at[offset], recv_sem=pair_recv.at[offset], device_id={"chan": partner},
+            src_ref=half_buf.at[offset, at, :], dst_ref=pair_buf.at[offset, at, :],
+            send_sem=pair_send.at[i], recv_sem=pair_recv.at[i], device_id={"chan": partner},
         )
         copy.start()
-        pair_copy[offset] = copy
-
-    depth = half_buf.shape[1] // PIECES
+        pair_copy[offset, piece] = copy
+
     arrived = set()
 
     def mine(offset, piece):
-        if offset not in arrived:
-            arrived.add(offset)
-            pair_copy[offset].wait_recv()
+        if (offset, piece) not in arrived:
+            arrived.add((offset, piece))
+            pair_copy[offset, piece].wait_recv()
         at = pl.ds(piece * depth, depth)
         tiles = TILES * 2 // PIECES
         part, begin = divmod(piece * tiles, TILES)
         own = canvas[part, pl.ds(begin, tiles), chan_rows(offset, core), :]
         return own.reshape(depth, LANES) + pair_buf[offset, at, :].astype(jnp.float32)
 
-    def length(piece, way):
-        return half - (piece + way) % 2
-
     ring = {}
 
-    def ring_step(step, every):
-        done = 0
+    def ring_step(step):
         for piece in range(PIECES):
             for way in range(2):
                 count = length(piece, way)
@@ -397,9 +405,6 @@
                 )
                 copy.start()
                 ring[way, piece, step] = copy
-                done += 1
-                if done % every == 0 and work:
-                    work.pop(0)()
 
     def degrid(begin):
         for s in range(begin, begin + DEGRIDS):
@@ -445,27 +450,28 @@
             place[s] = where
             place[subgrids + s] = before
 
-    work += [send_back, locate]
-    ring_step(0, 1)
+    ring_step(0)
+    pl.semaphore_wait(near_sem, len(near))
+    for peer in middle:
+        pl.semaphore_signal(far_sem, inc=1, device_id={"facet": peer})
     while work:
         work.pop(0)()
-    ring_step(1, 1)
-    ring_step(2, 1)
+    pl.semaphore_wait(far_sem, len(middle))
+    send_back()
+    locate()
+    for step in range(1, half):
+        ring_step(step)
     for copy in back_copy:
         copy.wait()
-    work += [functools.partial(degrid, s) for s in range(0, subgrids, DEGRIDS)]
-    ring_step(half - 1, 1)
+    for begin in range(0, subgrids, DEGRIDS):
+        degrid(begin)
     for piece in range(PIECES):
-        if work:
-            work.pop(0)()
         value = mine(0, piece)
         for way in range(2):
             step = length(piece, way) - 1
             ring[way, piece, step].wait_recv()
             value = value + recv_buf[(way * PIECES + piece) * half + step].astype(jnp.float32)
         total[pl.ds(piece * depth, depth), :] = value
-    while work:
-        work.pop(0)()
     for copy in pair_copy.values():
         copy.wait_send()
     for copy in ring.values():
@@ -578,13 +584,15 @@
             pltpu.VMEM((facets, SLOTS, SUB, LANES), jnp.bfloat16),
             pltpu.VMEM((facets, SLOTS, SUB, LANES), jnp.bfloat16),
             pltpu.SMEM((2 * subgrids,), jnp.int32),
-            pltpu.SemaphoreType.DMA((chips,)),
-            pltpu.SemaphoreType.DMA((chips,)),
+            pltpu.SemaphoreType.DMA((chips * PIECES,)),
+            pltpu.SemaphoreType.DMA((chips * PIECES,)),
             pltpu.SemaphoreType.DMA((links,)),
             pltpu.SemaphoreType.DMA((links,)),
             pltpu.SemaphoreType.DMA((facets,)),
             pltpu.SemaphoreType.DMA((facets,)),
             pltpu.SemaphoreType.DMA,
+            pltpu.SemaphoreType.REGULAR,
+            pltpu.SemaphoreType.REGULAR,
         ],
         compiler_params=pltpu.CompilerParams(
             collective_id=1, has_side_effects=True, vmem_limit_bytes=20 << 20

time: 41.8 us -> 41.7 us (level); the launches traced: 41 us -> 41.5 us
  Pallas kernels: 40.2 us -> 40.7 us
    pallas_call x1, Pallas kernels: 24.2 us -> 24.7 us  [per_device(): pl.pallas_call(functools.partial(exchange_kernel, facets, side, chans, su...]
where the time goes in v6:
time: 41.7 us; the launch traced here: 41.5 us
  Pallas kernels  40.7 us (98%)
  between operations  0.75 us (2%)
    pallas_call x1, Pallas kernels, per_device(): pl.pallas_call(functools.partial(exchange_kernel, facets, side, chans, su...  24.7 us
    pallas_call x1, Pallas kernels, per_device(): pl.pallas_call(functools.partial(grid_kernel, facets, side, subgrids), ou...  13.2 us
    pallas_call x1, Pallas kernels, per_device(): pl.pallas_call(functools.partial(add_kernel, facets), out_shape=shape((2,...  1.8 us
    pallas_call x1, Pallas kernels, per_device(): pl.pallas_call(functools.partial(output_kernel, rows), out_shape=(shape((...  0.98 us

profile of v6, /device:TPU:2, one launch (start us, length us, event | category | flops | bytes accessed | tf_op | source)
XLA Modules:
  0.0 41.5 jit_solution(563472961946673316)
XLA Ops:
  0.6 13.2 %grid_and_send.1 = (f32[2048,128]{1,0:T(8,128)S(1)}, s32[16,1,128]{2,1,0:T(1,128)S(1)}, f32[32,256,128]{2,1,0:T(8,128)S(1)}, f32[2,33,128,128]{3,2,1,0:T(8,128)S(1)}) custom-call(s32[16]{0:T(128)} %cnt.1, s32[16]{0:T(128)} %bitcast.1, s32[16]{0:T(128)} %row_hbm.1, s32[16]{0:T(128)} %col_hbm.1, f32[16,2,512]{2,1,0:T(2,128)} %vis.1, f32[16,2,512]{2,1,0:T(2,128)} %uv.1, ...), custom_call_target="tpu_custom_call" | custom-call | tf_op jit(solution)/shard_map/grid_and_send/pallas_call | solution.py:510
  13.9 0.0 copy-start
  13.9 0.0 copy-start.1
  13.9 0.0 copy-start.2
  13.9 0.0 copy-start.3
  13.9 0.0 copy-start.4
  13.9 0.0 copy-start.5
  14.0 1.8 %add_windows.1.canvas = f32[2,33,128,128]{3,2,1,0:T(8,128)S(1)} custom-call(s32[16,1,128]{2,1,0:T(1,128)S(1)} %get-tuple-element.8.meta, f32[2048,128]{1,0:T(8,128)S(1)} %get-tuple-element.9.patches, f32[2,33,128,128]{3,2,1,0:T(8,128)S(1)} %get-tuple-element.10._), custom_call_target="tpu_custom_call", output_to_operand_aliasing={{}: (2, {})} | custom-call | tf_op jit(solution)/shard_map/add_windows/pallas_call | solution.py:559
  15.8 0.0 copy-done
  15.8 0.0 copy-done.1
  15.8 0.0 copy-done.2
  15.8 0.0 copy-done.3
  15.8 0.0 copy-done.4
  15.8 0.0 copy-done.5
  15.8 24.7 %reduce_and_return.1 = (f32[512,128]{1,0:T(8,128)S(1)}, f32[16,2,512]{2,1,0:T(2,128)S(1)}) custom-call(s32[16,1,128]{2,1,0:T(1,128)S(1)} %get-tuple-element.8.meta, s32[16]{0:T(128)S(1)} %copy-done.4, s32[16]{0:T(128)S(1)} %bitcast.2, f32[2,33,128,128]{3,2,1,0:T(8,128)S(1)} %add_windows.1.canvas, f32[32,256,128]{2,1,0:T(8,128)S(1)} %get-tuple-element.11.model_rows, ...), custom_call_target="tpu_custom_call" | custom-call | tf_op jit(solution)/shard_map/reduce_and_return/pallas_call | solution.py:571
  40.5 1.0 %outputs.1 = (f32[1,8,2,4096]{3,2,1,0:T(2,128)}, f32[16,2,512]{2,1,0:T(2,128)}) custom-call(f32[512,128]{1,0:T(8,128)S(1)} %get-tuple-element.12.total, f32[16,2,512]{2,1,0:T(2,128)S(1)} %get-tuple-element.13.values), custom_call_target="tpu_custom_call" | custom-call | tf_op jit(solution)/shard_map/outputs/pallas_call | solution.py:603
Async XLA Ops:
  13.9 1.9 %copy-start = (f32[16,2,512]{2,1,0:T(2,128)S(1)}, f32[16,2,512]{2,1,0:T(2,128)}, u32[]{:S(2)}) copy-start(f32[16,2,512]{2,1,0:T(2,128)} %vis.1) | copy-start | bytes 196612
  13.9 1.9 %copy-start.1 = (f32[16,2,512]{2,1,0:T(2,128)S(1)}, f32[16,2,512]{2,1,0:T(2,128)}, u32[]{:S(2)}) copy-start(f32[16,2,512]{2,1,0:T(2,128)} %uv.1) | copy-start | bytes 196612
  13.9 1.9 %copy-start.2 = (bf16[128,128]{1,0:T(8,128)(2,1)S(1)}, bf16[128,128]{1,0:T(8,128)(2,1)}, u32[]{:S(2)}) copy-start(bf16[128,128]{1,0:T(8,128)(2,1)} %constant.11.clone.right_i) | copy-start | bytes 98308
  13.9 1.9 %copy-start.3 = (bf16[64,128]{1,0:T(8,128)(2,1)S(1)}, bf16[64,128]{1,0:T(8,128)(2,1)}, u32[]{:S(2)}) copy-start(bf16[64,128]{1,0:T(8,128)(2,1)} %constant.10.clone.left_i) | copy-start | bytes 49156
  13.9 1.9 %copy-start.4 = (s32[16]{0:T(128)S(1)}, s32[16]{0:T(128)}, u32[]{:S(2)}) copy-start(s32[16]{0:T(128)} %cnt.1) | copy-start | bytes 196
  13.9 1.9 %copy-start.5 = (s32[16,1]{0,1:T(1,128)S(1)}, s32[16,1]{0,1:T(1,128)}, u32[]{:S(2)}) copy-start(s32[16,1]{0,1:T(1,128)} %param.14) | copy-start | bytes 196

commit v7 on v6

--- a/solution.py
+++ b/solution.py
@@ -273,7 +273,7 @@
     facets, side, chans, subgrids,
     meta, cnt, fid, canvas, model_rows, vis, uv, left_i, right_i,
     total, residual,
-    half_buf, pair_buf, send_buf, recv_buf, back, returned, place,
+    own_ku, own_kv, half_buf, pair_buf, send_buf, recv_buf, back, returned, place,
     pair_send, pair_recv, ring_send, ring_recv, back_send, back_recv, own_sem, near_sem, far_sem,
 ):
     chips = chans // 2
@@ -406,11 +406,18 @@
                 copy.start()
                 ring[way, piece, step] = copy
 
+    def own_kernels(begin, end):
+        def one(s, carry):
+            own_ku[s] = kernel_low(uv[s, pl.ds(0, 1), :])
+            own_kv[s] = kernel_of(uv[s, pl.ds(1, 1), :])
+            return carry
+
+        lax.fori_loop(begin, end, one, 0, unroll=2)
+
     def degrid(begin):
         for s in range(begin, begin + DEGRIDS):
             image = returned[place[s], place[subgrids + s]]
-            ku = kernel_low(uv[s, pl.ds(0, 1), :])
-            weight = kernel_of(uv[s, pl.ds(1, 1), :])
+            ku, weight = own_ku[s], own_kv[s]
             inner = lax.dot_general(
                 image, ku, (((0,), (0,)), ((), ())), preferred_element_type=jnp.float32
             )
@@ -461,6 +468,8 @@
     locate()
     for step in range(1, half):
         ring_step(step)
+        if step < half - 1:
+            own_kernels((step - 1) * subgrids // 2, step * subgrids // 2)
     for copy in back_copy:
         copy.wait()
     for begin in range(0, subgrids, DEGRIDS):
@@ -577,6 +586,8 @@
         in_specs=[SMEM] * 3 + [VMEM] * 6,
         out_specs=(VMEM,) * 2,
         scratch_shapes=[
+            pltpu.VMEM((subgrids, SUB, NV), jnp.bfloat16),
+            pltpu.VMEM((subgrids, SUB, NV), jnp.float32),
             pltpu.VMEM((chips, 2 * TILES * rows, LANES), jnp.bfloat16),
             pltpu.VMEM((chips, 2 * TILES * rows, LANES), jnp.bfloat16),
             pltpu.VMEM((links, depth, LANES), jnp.bfloat16),

time: 41.7 us -> 41.7 us (level)
  no operation moved by 1% of the time
where the time goes in v7:
time: 41.7 us; the launch traced here: 41.5 us
  Pallas kernels  40.7 us (98%)
  between operations  0.75 us (2%)
    pallas_call x1, Pallas kernels, per_device(): pl.pallas_call(functools.partial(exchange_kernel, facets, side, chans, su...  24.7 us
    pallas_call x1, Pallas kernels, per_device(): pl.pallas_call(functools.partial(grid_kernel, facets, side, subgrids), ou...  13.2 us
    pallas_call x1, Pallas kernels, per_device(): pl.pallas_call(functools.partial(add_kernel, facets), out_shape=shape((2,...  1.8 us
    pallas_call x1, Pallas kernels, per_device(): pl.pallas_call(functools.partial(output_kernel, rows), out_shape=(shape((...  0.98 us

profile of v7, /device:TPU:2, one launch (start us, length us, event | category | flops | bytes accessed | tf_op | source)
XLA Modules:
  0.0 41.5 jit_solution(3342350451887750405)
XLA Ops:
  0.6 13.2 %grid_and_send.1 = (f32[2048,128]{1,0:T(8,128)S(1)}, s32[16,1,128]{2,1,0:T(1,128)S(1)}, f32[32,256,128]{2,1,0:T(8,128)S(1)}, f32[2,33,128,128]{3,2,1,0:T(8,128)S(1)}) custom-call(s32[16]{0:T(128)} %cnt.1, s32[16]{0:T(128)} %bitcast.1, s32[16]{0:T(128)} %row_hbm.1, s32[16]{0:T(128)} %col_hbm.1, f32[16,2,512]{2,1,0:T(2,128)} %vis.1, f32[16,2,512]{2,1,0:T(2,128)} %uv.1, ...), custom_call_target="tpu_custom_call" | custom-call | tf_op jit(solution)/shard_map/grid_and_send/pallas_call | solution.py:519
  13.9 0.0 copy-start
  13.9 0.0 copy-start.1
  13.9 0.0 copy-start.2
  13.9 0.0 copy-start.3
  13.9 0.0 copy-start.4
  13.9 0.0 copy-start.5
  14.0 1.8 %add_windows.1.canvas = f32[2,33,128,128]{3,2,1,0:T(8,128)S(1)} custom-call(s32[16,1,128]{2,1,0:T(1,128)S(1)} %get-tuple-element.8.meta, f32[2048,128]{1,0:T(8,128)S(1)} %get-tuple-element.9.patches, f32[2,33,128,128]{3,2,1,0:T(8,128)S(1)} %get-tuple-element.10._), custom_call_target="tpu_custom_call", output_to_operand_aliasing={{}: (2, {})} | custom-call | tf_op jit(solution)/shard_map/add_windows/pallas_call | solution.py:568
  15.8 0.0 copy-done
  15.8 0.0 copy-done.1
  15.8 0.0 copy-done.2
  15.8 0.0 copy-done.3
  15.8 0.0 copy-done.4
  15.8 0.0 copy-done.5
  15.8 24.7 %reduce_and_return.1 = (f32[512,128]{1,0:T(8,128)S(1)}, f32[16,2,512]{2,1,0:T(2,128)S(1)}) custom-call(s32[16,1,128]{2,1,0:T(1,128)S(1)} %get-tuple-element.8.meta, s32[16]{0:T(128)S(1)} %copy-done.4, s32[16]{0:T(128)S(1)} %bitcast.2, f32[2,33,128,128]{3,2,1,0:T(8,128)S(1)} %add_windows.1.canvas, f32[32,256,128]{2,1,0:T(8,128)S(1)} %get-tuple-element.11.model_rows, ...), custom_call_target="tpu_custom_call" | custom-call | tf_op jit(solution)/shard_map/reduce_and_return/pallas_call | solution.py:580
  40.5 1.0 %outputs.1 = (f32[1,8,2,4096]{3,2,1,0:T(2,128)}, f32[16,2,512]{2,1,0:T(2,128)}) custom-call(f32[512,128]{1,0:T(8,128)S(1)} %get-tuple-element.12.total, f32[16,2,512]{2,1,0:T(2,128)S(1)} %get-tuple-element.13.values), custom_call_target="tpu_custom_call" | custom-call | tf_op jit(solution)/shard_map/outputs/pallas_call | solution.py:614
Async XLA Ops:
  13.9 1.9 %copy-start = (f32[16,2,512]{2,1,0:T(2,128)S(1)}, f32[16,2,512]{2,1,0:T(2,128)}, u32[]{:S(2)}) copy-start(f32[16,2,512]{2,1,0:T(2,128)} %vis.1) | copy-start | bytes 196612
  13.9 1.9 %copy-start.1 = (f32[16,2,512]{2,1,0:T(2,128)S(1)}, f32[16,2,512]{2,1,0:T(2,128)}, u32[]{:S(2)}) copy-start(f32[16,2,512]{2,1,0:T(2,128)} %uv.1) | copy-start | bytes 196612
  13.9 1.9 %copy-start.2 = (bf16[128,128]{1,0:T(8,128)(2,1)S(1)}, bf16[128,128]{1,0:T(8,128)(2,1)}, u32[]{:S(2)}) copy-start(bf16[128,128]{1,0:T(8,128)(2,1)} %constant.11.clone.right_i) | copy-start | bytes 98308
  13.9 1.9 %copy-start.3 = (bf16[64,128]{1,0:T(8,128)(2,1)S(1)}, bf16[64,128]{1,0:T(8,128)(2,1)}, u32[]{:S(2)}) copy-start(bf16[64,128]{1,0:T(8,128)(2,1)} %constant.10.clone.left_i) | copy-start | bytes 49156
  13.9 1.9 %copy-start.4 = (s32[16]{0:T(128)S(1)}, s32[16]{0:T(128)}, u32[]{:S(2)}) copy-start(s32[16]{0:T(128)} %cnt.1) | copy-start | bytes 196
  13.9 1.9 %copy-start.5 = (s32[16,1]{0,1:T(1,128)S(1)}, s32[16,1]{0,1:T(1,128)}, u32[]{:S(2)}) copy-start(s32[16,1]{0,1:T(1,128)} %param.14) | copy-start | bytes 196

commit v8 on v7

--- a/solution.py
+++ b/solution.py
@@ -261,7 +261,7 @@
                 )
         return carry
 
-    lax.fori_loop(0, facets, add, 0, unroll=2)
+    lax.fori_loop(0, facets, add, 0, unroll=4)
 
 
 PIECES = 4
@@ -487,16 +487,26 @@
         copy.wait_send()
 
 
-def output_kernel(rows, total, values, image, residual):
+def output_kernel(rows, total, values, image, residual, held, sem):
+    copies = [pltpu.make_async_copy(values, residual, sem.at[0])]
+    copies[0].start()
+    span = TILES // 4
+
     def place(tile, carry):
         at = pl.ds(pl.multiple_of(tile * LANES, LANES), LANES)
         for part in range(2):
             begin = pl.multiple_of((part * TILES + tile) * rows, rows)
-            image[0, :, part, at] = total[pl.ds(begin, rows), :]
+            held[0, :, part, at] = total[pl.ds(begin, rows), :]
         return carry
 
-    lax.fori_loop(0, TILES, place, 0, unroll=4)
-    residual[...] = values[...]
+    for chunk in range(4):
+        lax.fori_loop(chunk * span, (chunk + 1) * span, place, 0, unroll=4)
+        at = pl.ds(chunk * span * LANES, span * LANES)
+        copy = pltpu.make_async_copy(held.at[:, :, :, at], image.at[:, :, :, at], sem.at[chunk + 1])
+        copy.start()
+        copies.append(copy)
+    for copy in copies:
+        copy.wait()
 
 
 VMEM = pl.BlockSpec(memory_space=pltpu.VMEM)
@@ -618,7 +628,11 @@
             shape(visibility.shape, jnp.float32),
         ),
         in_specs=[VMEM] * 2,
-        out_specs=(VMEM,) * 2,
+        out_specs=(HBM,) * 2,
+        scratch_shapes=[
+            pltpu.VMEM((1, rows, 2, FACET), jnp.float32),
+            pltpu.SemaphoreType.DMA((5,)),
+        ],
         compiler_params=pltpu.CompilerParams(vmem_limit_bytes=8 << 20),
         name="outputs",
     )(total, residual)

time: 41.7 us -> 41.3 us (level)
  no operation moved by 1% of the time
where the time goes in v8:
time: 41.3 us; the launch traced here: 41.2 us
  Pallas kernels  40.4 us (98%)
  between operations  0.75 us (2%)
    pallas_call x1, Pallas kernels, per_device(): pl.pallas_call(functools.partial(exchange_kernel, facets, side, chans, su...  24.7 us
    pallas_call x1, Pallas kernels, per_device(): pl.pallas_call(functools.partial(grid_kernel, facets, side, subgrids), ou...  13.2 us
    pallas_call x1, Pallas kernels, per_device(): pl.pallas_call(functools.partial(add_kernel, facets), out_shape=shape((2,...  1.51 us
    pallas_call x1, Pallas kernels, per_device(): pl.pallas_call(functools.partial(output_kernel, rows), out_shape=(shape((...  0.93 us

profile of v8, /device:TPU:2, one launch (start us, length us, event | category | flops | bytes accessed | tf_op | source)
XLA Modules:
  0.0 41.2 jit_solution(14181838829934643295)
XLA Ops:
  0.6 13.2 %grid_and_send.1 = (f32[2048,128]{1,0:T(8,128)S(1)}, s32[16,1,128]{2,1,0:T(1,128)S(1)}, f32[32,256,128]{2,1,0:T(8,128)S(1)}, f32[2,33,128,128]{3,2,1,0:T(8,128)S(1)}) custom-call(s32[16]{0:T(128)} %cnt.1, s32[16]{0:T(128)} %bitcast.1, s32[16]{0:T(128)} %row_hbm.1, s32[16]{0:T(128)} %col_hbm.1, f32[16,2,512]{2,1,0:T(2,128)} %vis.1, f32[16,2,512]{2,1,0:T(2,128)} %uv.1, ...), custom_call_target="tpu_custom_call" | custom-call | tf_op jit(solution)/shard_map/grid_and_send/pallas_call | solution.py:529
  13.9 0.0 copy-start
  13.9 0.0 copy-start.1
  13.9 0.0 copy-start.2
  13.9 0.0 copy-start.3
  13.9 0.0 copy-start.4
  13.9 0.0 copy-start.5
  14.0 1.5 %add_windows.1.canvas = f32[2,33,128,128]{3,2,1,0:T(8,128)S(1)} custom-call(s32[16,1,128]{2,1,0:T(1,128)S(1)} %get-tuple-element.8.meta, f32[2048,128]{1,0:T(8,128)S(1)} %get-tuple-element.9.patches, f32[2,33,128,128]{3,2,1,0:T(8,128)S(1)} %get-tuple-element.10._), custom_call_target="tpu_custom_call", output_to_operand_aliasing={{}: (2, {})} | custom-call | tf_op jit(solution)/shard_map/add_windows/pallas_call | solution.py:578
  15.5 0.0 copy-done
  15.5 0.0 copy-done.1
  15.5 0.0 copy-done.2
  15.5 0.0 copy-done.3
  15.5 0.0 copy-done.4
  15.5 0.0 copy-done.5
  15.5 24.7 %reduce_and_return.1 = (f32[512,128]{1,0:T(8,128)S(1)}, f32[16,2,512]{2,1,0:T(2,128)S(1)}) custom-call(s32[16,1,128]{2,1,0:T(1,128)S(1)} %get-tuple-element.8.meta, s32[16]{0:T(128)S(1)} %copy-done.4, s32[16]{0:T(128)S(1)} %bitcast.2, f32[2,33,128,128]{3,2,1,0:T(8,128)S(1)} %add_windows.1.canvas, f32[32,256,128]{2,1,0:T(8,128)S(1)} %get-tuple-element.11.model_rows, ...), custom_call_target="tpu_custom_call" | custom-call | tf_op jit(solution)/shard_map/reduce_and_return/pallas_call | solution.py:590
  40.3 0.9 %outputs.1 = (f32[1,8,2,4096]{3,2,1,0:T(2,128)}, f32[16,2,512]{2,1,0:T(2,128)}) custom-call(f32[512,128]{1,0:T(8,128)S(1)} %get-tuple-element.12.total, f32[16,2,512]{2,1,0:T(2,128)S(1)} %get-tuple-element.13.values), custom_call_target="tpu_custom_call" | custom-call | tf_op jit(solution)/shard_map/outputs/pallas_call | solution.py:624
Async XLA Ops:
  13.9 1.6 %copy-start = (f32[16,2,512]{2,1,0:T(2,128)S(1)}, f32[16,2,512]{2,1,0:T(2,128)}, u32[]{:S(2)}) copy-start(f32[16,2,512]{2,1,0:T(2,128)} %vis.1) | copy-start | bytes 196612
  13.9 1.6 %copy-start.1 = (f32[16,2,512]{2,1,0:T(2,128)S(1)}, f32[16,2,512]{2,1,0:T(2,128)}, u32[]{:S(2)}) copy-start(f32[16,2,512]{2,1,0:T(2,128)} %uv.1) | copy-start | bytes 196612
  13.9 1.6 %copy-start.2 = (bf16[128,128]{1,0:T(8,128)(2,1)S(1)}, bf16[128,128]{1,0:T(8,128)(2,1)}, u32[]{:S(2)}) copy-start(bf16[128,128]{1,0:T(8,128)(2,1)} %constant.11.clone.right_i) | copy-start | bytes 98308
  13.9 1.6 %copy-start.3 = (bf16[64,128]{1,0:T(8,128)(2,1)S(1)}, bf16[64,128]{1,0:T(8,128)(2,1)}, u32[]{:S(2)}) copy-start(bf16[64,128]{1,0:T(8,128)(2,1)} %constant.10.clone.left_i) | copy-start | bytes 49156
  13.9 1.6 %copy-start.4 = (s32[16]{0:T(128)S(1)}, s32[16]{0:T(128)}, u32[]{:S(2)}) copy-start(s32[16]{0:T(128)} %cnt.1) | copy-start | bytes 196
  13.9 1.6 %copy-start.5 = (s32[16,1]{0,1:T(1,128)S(1)}, s32[16,1]{0,1:T(1,128)}, u32[]{:S(2)}) copy-start(s32[16,1]{0,1:T(1,128)} %param.14) | copy-start | bytes 196
